TPU v7x, 256 devices: a whole 4x4x8 slice. The times are simulated.
256 devices in a mesh: freq: 8 (over y, core), stcol: 32 (over x, z).
Axes of the slice: x: 4, y: 4, z: 8, core: 2. Of those that a mesh axis runs over, the one named last changes fastest.
Arguments:
- visibilities: float32 [2, 8, 512, 1, 512], P(None, 'freq', 'stcol'), may hold values from -28.8 to 28.8
- positions: float32 [3, 1, 512], replicated, may hold values from -3 to 3
- source_lmn: float32 [3, 1024], replicated, may hold values from -0.5 to 0.5
- source_flux: float32 [1024], replicated, may hold values from 0.02 to 0.2
- cluster_map: int32 [1024], replicated, may hold values from 0 to 15, as said below
- station_order: int32 [512], replicated, may hold values from 0 to 511, each once
- penalty: float32 [16], replicated, may hold values from 9.8304 to 196.608
- offsets: float32 [2, 8, 16, 512], P(None, 'freq'), may hold values from -1.2 to 1.2
Outputs:
- gains: float32 [2, 8, 16, 512], P(None, 'freq', None, 'stcol')
- consensus: float32 [2, 8, 16, 512], P(None, 'freq', None, 'stcol')
Inputs may be any that keep to these rules, and one draw needn't show every extreme that they name: `cluster_map`: each of the 16 directions is named by exactly 64 sources. `station_order`: every station stands exactly once.
All inputs are finite; a program needn't handle non-finite values.
Results may differ from a plain program's by a relative error of at most 0.00011.
Values sent between devices are 32-bit elements; how exact they have to be, the bound alone decides.
No kernel may reach another device: no remote copies, remote signals or barrier semaphores. Data moves between devices by JAX's collectives and lax.ppermute only.
A program may use at most 64 MiB of HBM per device.

v0:
```python
import math

import jax
import jax.numpy as jnp
from jax import lax
from jax.sharding import PartitionSpec as P

ADMM = 2
PASSES = 2


HIGHEST = lax.Precision.HIGHEST


def copy_for_each(x, axis):
    copies = jnp.broadcast_to(x, (lax.axis_size(axis), *x.shape))
    return lax.all_to_all(copies, axis, split_axis=0, concat_axis=0, tiled=True)


def in_order(tiles, dim):
    shape = list(tiles.shape[1:])
    shape[dim] *= tiles.shape[0]
    return jnp.moveaxis(tiles, 0, dim).reshape(shape)


def gather_directly(x, axis, dim):
    tiles = copy_for_each(x, axis)
    return in_order(tiles, dim)


def in_blocks(x, dim, count):
    shape = x.shape
    tiles = x.reshape(*shape[:dim], count, shape[dim] // count, *shape[dim + 1 :])
    return jnp.moveaxis(tiles, dim, 0)


def sent_and_summed(x, axis, dim):
    count = lax.axis_size(axis)
    tiles = lax.all_to_all(in_blocks(x, dim, count), axis, 0, 0, tiled=True)
    return jnp.sum(tiles, axis=0)


def sent_together(arrays, axis, dim, along):
    widths = [a.shape[along] for a in arrays]
    both = jnp.concatenate(arrays, axis=along)
    filled = sent_and_summed(both, axis, dim)
    return tuple(jnp.split(filled, [sum(widths[:k]) for k in range(1, len(widths))], axis=along))


def frequencies(channels):
    return 1.0 + 0.5 * jnp.arange(channels, dtype=jnp.float32) / channels


def basis_table(channels):
    centre = (jnp.arange(channels, dtype=jnp.float32) - 0.5 * (channels - 1)) / channels
    columns = [jnp.ones_like(centre), centre, centre * centre]
    finished = []
    for column in columns:
        for before in finished:
            column = column - jnp.sum(column * before) * before
        finished.append(column / jnp.sqrt(jnp.sum(column * column)))
    return jnp.stack(finished, axis=1)


def group_sources(source_lmn, source_flux, cluster_map, directions):
    ranking = jnp.argsort(cluster_map, stable=True)
    cosines = jnp.take(source_lmn, ranking, axis=1).reshape(3, directions, -1)
    brightness = jnp.take(source_flux, ranking).reshape(directions, -1)
    return (jnp.moveaxis(cosines, 1, 0), brightness)


def contract(row_part, column_part):
    return jnp.einsum("ctps,ctjs->cjtp", row_part, column_part, precision=HIGHEST)


def model_block(positions, direction_cosines, weights, freq_scale, column_ids):
    projected = (
        positions[0][:, :, None] * direction_cosines[0]
        + positions[1][:, :, None] * direction_cosines[1]
    )
    projected = projected + positions[2][:, :, None] * direction_cosines[2]
    phases = 2.0 * math.pi * freq_scale[:, None, None, None] * projected[None]
    cosine = jnp.cos(phases)
    sine_part = jnp.sin(phases)
    weighted_cos = cosine * weights
    weighted_sin = sine_part * weights
    column_cos = jnp.take(cosine, column_ids, axis=2)
    column_sin = jnp.take(sine_part, column_ids, axis=2)
    model_real = contract(weighted_cos, column_cos) + contract(weighted_sin, column_sin)
    model_imag = contract(weighted_sin, column_cos) - contract(weighted_cos, column_sin)
    station_ids = jnp.arange(positions.shape[2], dtype=jnp.int32)
    retained = (column_ids[:, None] != station_ids[None, :]).astype(model_real.dtype)
    retained = retained[None, :, None, :]
    return (model_real * retained, model_imag * retained)


def build_models(positions, cosines, brightness, freq_scale, column_ids):

    def one_model(entry):
        return model_block(positions, entry[0], entry[1], freq_scale, column_ids)

    return lax.map(one_model, (cosines, brightness))


def gain_update(numerator, denominator, gains, consensus, multiplier, penalty):
    weight_pen = penalty[:, None]
    scaling = 1.0 / (denominator + weight_pen)
    fresh = (numerator + gains * denominator + weight_pen * (consensus - multiplier)) * scaling
    return 0.5 * (gains + fresh)


def pass_terms(visibilities, gains, model_real, model_imag, column_ids):
    column_gains = jnp.take(gains, column_ids, axis=3)
    column_real = jnp.moveaxis(column_gains[0], 1, 0)[:, :, :, None, None]
    column_imag = jnp.moveaxis(column_gains[1], 1, 0)[:, :, :, None, None]
    row_real = jnp.moveaxis(gains[0], 1, 0)[:, :, None, None, :]
    row_imag = jnp.moveaxis(gains[1], 1, 0)[:, :, None, None, :]
    along_real = model_real * column_real + model_imag * column_imag
    along_imag = model_imag * column_real - model_real * column_imag
    pred_real = row_real * along_real - row_imag * along_imag
    pred_imag = row_real * along_imag + row_imag * along_real
    resid_real = visibilities[0] - jnp.sum(pred_real, axis=0)
    resid_imag = visibilities[1] - jnp.sum(pred_imag, axis=0)
    num_real = jnp.sum(resid_real * along_real + resid_imag * along_imag, axis=(2, 3))
    num_imag = jnp.sum(resid_imag * along_real - resid_real * along_imag, axis=(2, 3))
    denominator = jnp.sum(along_real * along_real + along_imag * along_imag, axis=(2, 3))
    numerator = jnp.moveaxis(jnp.stack([num_real, num_imag]), 1, 2)
    return (numerator, jnp.moveaxis(denominator, 0, 1)[None])


def channel_fit(values, local_basis, basis):
    all_channels = gather_directly(values, "freq", 1)
    coefficients = jnp.einsum("fj,rfkp->rjkp", basis, all_channels, precision=HIGHEST)
    return jnp.einsum("fj,rjkp->rfkp", local_basis, coefficients, precision=HIGHEST)


def on_device(
    visibilities, positions, source_lmn, source_flux, cluster_map, station_order, penalty, offsets
):
    chan_dev = visibilities.shape[1]
    column_count = visibilities.shape[2]
    stations = visibilities.shape[4]
    directions = penalty.shape[0]
    channels = chan_dev * lax.axis_size("freq")
    row_index = lax.axis_index("freq")
    col_index = lax.axis_index("stcol")
    owned_count = stations // lax.axis_size("stcol")
    column_ids = lax.dynamic_slice_in_dim(station_order, col_index * column_count, column_count)
    freq_scale = lax.dynamic_slice_in_dim(frequencies(channels), row_index * chan_dev, chan_dev)
    basis = basis_table(channels)
    local_basis = lax.dynamic_slice_in_dim(basis, row_index * chan_dev, chan_dev, 0)
    cosines, brightness = group_sources(source_lmn, source_flux, cluster_map, directions)
    model_real, model_imag = build_models(positions, cosines, brightness, freq_scale, column_ids)
    gains = jnp.stack([1.0 + offsets[0], offsets[1]])
    owned = lax.dynamic_slice_in_dim(gains, col_index * owned_count, owned_count, 3)
    consensus = owned
    multiplier = jnp.zeros_like(owned)
    for admm_step in range(ADMM):
        for sweep_index in range(PASSES):
            numerator, denominator = pass_terms(
                visibilities, gains, model_real, model_imag, column_ids
            )
            numerator, denominator = sent_together((numerator, denominator), "stcol", 3, 0)
            owned = gain_update(numerator, denominator, owned, consensus, multiplier, penalty)
            if admm_step * PASSES + sweep_index + 1 < ADMM * PASSES:
                gains = gather_directly(owned, "stcol", 3)
        consensus = channel_fit(owned + multiplier, local_basis, basis)
        multiplier = multiplier + owned - consensus
    return (owned, consensus)


def solution(mesh):
    in_specs = (
        P(None, "freq", "stcol", None, None),
        P(),
        P(),
        P(),
        P(),
        P(),
        P(),
        P(None, "freq", None, None),
    )
    out_specs = (P(None, "freq", None, "stcol"), P(None, "freq", None, "stcol"))
    return jax.shard_map(
        on_device, mesh=mesh, in_specs=in_specs, out_specs=out_specs, check_vma=False
    )
```

profile of v0, /device:TPU:1, one launch (start us, length us, event | category | flops | bytes accessed | tf_op | source)
XLA Modules:
  0.0 292.0 jit_solution(11313309045373092982)
XLA Ops:
  1.3 4.4 %sort.17 = (s32[1024]{0:T(1024)}, s32[1024]{0:T(1024)S(1)}) sort(s32[1024]{0:T(1024)S(1)} %copy-done.5, s32[1024]{0:T(1024)S(1)} %iota.29), dimensions={0}, to_apply=%region_0.0 | sort | flops 10240 | bytes 16384 | tf_op jit(solution)/shard_map/jit(argsort)/sort | solution.py:66
  9.3 2.8 gather_fusion.2
  12.4 4.5 %gather_fusion.3 = f32[1024]{0:T(1024)S(1)} fusion(f32[1024]{0:T(1024)S(1)} %copy-done, s32[1024]{0:T(1024)S(1)} %fusion.81), kind=kCustom, calls=%fused_computation.7 | custom fusion | bytes 12288 | tf_op jit(solution)/shard_map/jit(_take)/gather | solution.py:68
  18.3 121.1 %while.14 = (s32[]{:T(128)}, f32[16,1,16,1,512]{4,2,3,1,0:T(8,128)S(1)}, f32[16,1,16,1,512]{4,2,3,1,0:T(8,128)S(1)}, s32[16]{0:T(128)S(1)}, f32[1,1,1,1]{3,2,1,0...) while((s32[]{:T(128)}, ...), condition=%wide.region_2.4_spmd, body=%wide.region_1.3_spmd.sunk | while | flops 26334352 | bytes 559921 | solution.py:102
  24.6 1.3 fusion.122
  47.3 1.3 fusion.122
  62.4 1.3 fusion.122
  77.5 1.3 fusion.122
  100.2 1.3 fusion.122
  115.4 1.3 fusion.122
  138.1 1.3 fusion.122
  142.0 20.7 %all_to_all.45 = f32[32,1,768]{2,1,0:T(1,128)S(1)} all-to-all(f32[32,1,768]{2,1,0:T(1,128)S(1)} %reshape.1139), channel_id=1, replica_groups=mesh['freq'=8,'stcol'=32] {'stcol'}, dimensions={0} | all-to-all | bytes 196608 | tf_op jit(solution)/shard_map/all_to_all | solution.py:39
  165.4 12.1 %all_to_all.46 = f32[32,1,512]{2,1,0:T(1,128)S(1)} all-to-all(f32[32,1,512]{2,1,0:T(1,128)S(1)} %reshape.1141), channel_id=1, replica_groups=mesh['freq'=8,'stcol'=32] {'stcol'}, dimensions={0} | all-to-all | bytes 131072 | tf_op jit(solution)/shard_map/all_to_all | solution.py:17
  182.8 3.9 %all-to-all-start.2 = ((f32[32,1,768]{2,1,0:T(1,128)}), f32[32,1,768]{2,1,0:T(1,128)S(1)}, u32[]{:S(2)}, u32[]{:S(2)}) async-start(f32[32,1,768]{2,1,0:T(1,128)} %reshape.1143), calls=%async_computation.2 | async-start | bytes 196608 | tf_op jit(solution)/shard_map/all_to_all | solution.py:39
  193.8 2.0 all-to-all-done.2
  197.8 8.9 %all-to-all-start.5 = ((f32[8,1,512]{2,1,0:T(1,128)}), f32[8,1,512]{2,1,0:T(1,128)S(1)}, u32[]{:S(2)}, u32[]{:S(2)}) async-start(f32[8,1,512]{2,1,0:T(1,128)} %reshape.1149), calls=%async_computation.5 | async-start | bytes 32768 | tf_op jit(solution)/shard_map/all_to_all | solution.py:17
  207.9 3.5 %all-to-all-done.5 = f32[8,1,512]{2,1,0:T(1,128)S(1)} async-done(((f32[8,1,512]{2,1,0:T(1,128)}), f32[8,1,512]{2,1,0:T(1,128)S(1)}, u32[]{:S(2)}, u32[]{:S(2)}) %all-to-all-start.5) | async-done | bytes 16416 | tf_op jit(solution)/shard_map/all_to_all | solution.py:17
  211.4 6.4 %all-to-all-start.3 = ((f32[32,1,512]{2,1,0:T(1,128)}), f32[32,1,512]{2,1,0:T(1,128)S(1)}, u32[]{:S(2)}, u32[]{:S(2)}) async-start(f32[32,1,512]{2,1,0:T(1,128)} %reshape.1145), calls=%async_computation.3 | async-start | bytes 131072 | tf_op jit(solution)/shard_map/all_to_all | solution.py:17
  218.8 7.8 %all-to-all-done.3 = f32[32,1,512]{2,1,0:T(1,128)S(1)} async-done(((f32[32,1,512]{2,1,0:T(1,128)}), f32[32,1,512]{2,1,0:T(1,128)S(1)}, u32[]{:S(2)}, u32[]{:S(2)}) %all-to-all-start.3) | async-done | bytes 65568 | tf_op jit(solution)/shard_map/all_to_all | solution.py:17
  231.9 3.9 %all-to-all-start.4 = ((f32[32,1,768]{2,1,0:T(1,128)}), f32[32,1,768]{2,1,0:T(1,128)S(1)}, u32[]{:S(2)}, u32[]{:S(2)}) async-start(f32[32,1,768]{2,1,0:T(1,128)} %reshape.1147), calls=%async_computation.4 | async-start | bytes 196608 | tf_op jit(solution)/shard_map/all_to_all | solution.py:39
  236.0 8.8 %all-to-all-done.4 = f32[32,1,768]{2,1,0:T(1,128)S(1)} async-done(((f32[32,1,768]{2,1,0:T(1,128)}), f32[32,1,768]{2,1,0:T(1,128)S(1)}, u32[]{:S(2)}, u32[]{:S(2)}) %all-to-all-start.4) | async-done | bytes 98336 | tf_op jit(solution)/shard_map/all_to_all | solution.py:39
  246.4 12.1 %all_to_all.47 = f32[32,1,512]{2,1,0:T(1,128)S(1)} all-to-all(f32[32,1,512]{2,1,0:T(1,128)S(1)} %reshape.1151), channel_id=1, replica_groups=mesh['freq'=8,'stcol'=32] {'stcol'}, dimensions={0} | all-to-all | bytes 131072 | tf_op jit(solution)/shard_map/all_to_all | solution.py:17
  263.2 12.1 %all_to_all.48 = f32[32,1,768]{2,1,0:T(1,128)S(1)} all-to-all(f32[32,1,768]{2,1,0:T(1,128)S(1)} %reshape.1153), channel_id=1, replica_groups=mesh['freq'=8,'stcol'=32] {'stcol'}, dimensions={0} | all-to-all | bytes 196608 | tf_op jit(solution)/shard_map/all_to_all | solution.py:39
  277.3 12.7 %all_to_all.49 = f32[8,1,512]{2,1,0:T(1,128)S(1)} all-to-all(f32[8,1,512]{2,1,0:T(1,128)S(1)} %reshape.1155), channel_id=1, replica_groups=mesh['freq'=8,'stcol'=32] {'freq'}, dimensions={0} | all-to-all | bytes 32768 | tf_op jit(solution)/shard_map/all_to_all | solution.py:17
  (384 shorter events, 149.6 us)
Async XLA Ops:
  0.6 11.8 %copy-start = (f32[1024]{0:T(1024)S(1)}, f32[1024]{0:T(1024)}, u32[]{:S(2)}) copy-start(f32[1024]{0:T(1024)} %param.17) | copy-start | bytes 12292
  0.6 0.7 copy-start.5
  8.3 0.7 copy-start.4
  17.0 1.3 copy-start.2
  139.4 0.8 copy-start.1
  164.3 0.7 copy-start.3
  182.8 12.9 %all-to-all-start.2 = ((f32[32,1,768]{2,1,0:T(1,128)}), f32[32,1,768]{2,1,0:T(1,128)S(1)}, u32[]{:S(2)}, u32[]{:S(2)}) async-start(f32[32,1,768]{2,1,0:T(1,128)} %reshape.1143), calls=%async_computation.2 | async-start | bytes 196608 | tf_op jit(solution)/shard_map/all_to_all | solution.py:39
  197.8 13.6 %all-to-all-start.5 = ((f32[8,1,512]{2,1,0:T(1,128)}), f32[8,1,512]{2,1,0:T(1,128)S(1)}, u32[]{:S(2)}, u32[]{:S(2)}) async-start(f32[8,1,512]{2,1,0:T(1,128)} %reshape.1149), calls=%async_computation.5 | async-start | bytes 32768 | tf_op jit(solution)/shard_map/all_to_all | solution.py:17
  211.4 15.3 %all-to-all-start.3 = ((f32[32,1,512]{2,1,0:T(1,128)}), f32[32,1,512]{2,1,0:T(1,128)S(1)}, u32[]{:S(2)}, u32[]{:S(2)}) async-start(f32[32,1,512]{2,1,0:T(1,128)} %reshape.1145), calls=%async_computation.3 | async-start | bytes 131072 | tf_op jit(solution)/shard_map/all_to_all | solution.py:17
  231.9 12.9 %all-to-all-start.4 = ((f32[32,1,768]{2,1,0:T(1,128)}), f32[32,1,768]{2,1,0:T(1,128)S(1)}, u32[]{:S(2)}, u32[]{:S(2)}) async-start(f32[32,1,768]{2,1,0:T(1,128)} %reshape.1147), calls=%async_computation.4 | async-start | bytes 196608 | tf_op jit(solution)/shard_map/all_to_all | solution.py:39
where the time goes:
time: 293 us; the launch traced here: 292 us
  matrix products  85.7 us (29%)
  blocking collectives  69.8 us (24%)
  local copies, waits for them, and re-layouts  45.9 us (16%)
  other arithmetic  39 us (13%)
  starting transfers between devices  23 us (8%)
  waiting for transfers between devices  22 us (8%)
  between operations  4.85 us (2%)
    dot_general x64, matrix products, contract(): jnp.einsum('ctps,ctjs->cjtp', row_part, column_part, precision=HIGHEST)  83.9 us
    all_to_all x3, blocking collectives, copy_for_each(): return lax.all_to_all(copies, axis, split_axis=0, concat_axis=0, tiled=True)  37 us
    all_to_all x2, blocking collectives, sent_and_summed(): tiles = lax.all_to_all(in_blocks(x, dim, count), axis, 0, 0, tiled=True)  32.8 us
    another operation x16, other arithmetic, model_block(): column_sin = jnp.take(sine_part, column_ids, axis=2)  16.5 us
    all_to_all x2, starting transfers between devices, copy_for_each(): return lax.all_to_all(copies, axis, split_axis=0, concat_axis=0, tiled=True)  15.3 us
    all_to_all x2, waiting for transfers between devices, copy_for_each(): return lax.all_to_all(copies, axis, split_axis=0, concat_axis=0, tiled=True)  11.3 us
    all_to_all x2, waiting for transfers between devices, sent_and_summed(): tiles = lax.all_to_all(in_blocks(x, dim, count), axis, 0, 0, tiled=True)  10.7 us
    unnamed x40, local copies, waits for them, and re-layouts  9.25 us
  transfers between devices with their start and end apart: 4, of which 4 were waited for; matrix products, arithmetic and copies ran while one was open for 2% of the time, Pallas kernels for 0%

commit v1 on v0

v1 whole, which is shorter than its diff:
```python
import math

import jax
import jax.numpy as jnp
import numpy as np
from jax import lax
from jax.experimental import pallas as pl
from jax.experimental.pallas import tpu as pltpu
from jax.sharding import PartitionSpec as P

STATIONS = 512
DIRS = 16
SRC = 64
CHANNELS = 8
GROUP = 32
OWN = 16
LANES = 128
F32 = jnp.float32
BF16 = jnp.bfloat16

COS_TERMS = None
SIN_TERMS = None


def fit_terms():
    nodes = np.cos(np.pi * (np.arange(400) + 0.5) / 400)
    u = 0.125 * (nodes + 1.0)
    r = np.sqrt(u)
    cheb = np.polynomial.chebyshev
    poly = np.polynomial.polynomial

    def terms(values, degree):
        series = cheb.cheb2poly(cheb.chebfit(nodes, values, degree))
        out = np.zeros(1)
        for c in series[::-1]:
            out = poly.polyadd(poly.polymul(out, [-1.0, 8.0]), [c])
        return [float(np.float32(c)) for c in out[: degree + 1]]

    return terms(np.cos(2 * np.pi * r), 7), terms(np.sin(2 * np.pi * r) / r, 6)


COS_TERMS, SIN_TERMS = fit_terms()


def basis_table():
    centre = (np.arange(CHANNELS) - 0.5 * (CHANNELS - 1)) / CHANNELS
    columns = [np.ones_like(centre), centre, centre * centre]
    finished = []
    for column in columns:
        for before in finished:
            column = column - np.sum(column * before) * before
        finished.append(column / np.sqrt(np.sum(column * column)))
    return np.stack(finished, axis=1)


BASIS = basis_table()


def channel_weights(channel):
    centre = (np.arange(CHANNELS) - 0.5 * (CHANNELS - 1)) / CHANNELS
    square = centre * centre
    flat = BASIS[:, 0]
    lift = float(np.sum(square * flat))
    norm1 = float(np.sqrt(np.sum(centre * centre)))
    norm2 = float(np.sqrt(np.sum((square - lift * flat) ** 2)))
    x = (channel.astype(F32) - 0.5 * (CHANNELS - 1)) * (1.0 / CHANNELS)
    row = (float(flat[0]), x * (1.0 / norm1), (x * x - lift * float(flat[0])) * (1.0 / norm2))
    return [sum(row[j] * float(BASIS[f, j]) for j in range(3)) for f in range(CHANNELS)]


def horner(u, terms):
    out = jnp.full_like(u, terms[-1])
    for c in terms[-2::-1]:
        out = out * u + c
    return out


def wrapped(turns):
    return turns - jnp.round(turns)


def cos_turns(r):
    return horner(r * r, COS_TERMS)


def sin_turns(r):
    return r * horner(r * r, SIN_TERMS)


def split2(x):
    high = x.astype(BF16)
    return high, (x - high.astype(F32)).astype(BF16)


def split3(x):
    high = x.astype(BF16)
    rest = x - high.astype(F32)
    mid = rest.astype(BF16)
    return high, mid, (rest - mid.astype(F32)).astype(BF16)


def dot(a, b):
    return lax.dot_general(a, b, (((1,), (0,)), ((), ())), preferred_element_type=F32)


def dot_nt(a, b):
    return lax.dot_general(a, b, (((1,), (1,)), ((), ())), preferred_element_type=F32)


def chosen(pieces, table):
    return dot_nt(pieces[2], table) + dot_nt(pieces[1], table) + dot_nt(pieces[0], table)


def iota(shape, dim):
    return lax.broadcasted_iota(jnp.int32, shape, dim)


def as_table(cond):
    return jnp.where(cond, jnp.ones(cond.shape, F32), jnp.zeros(cond.shape, F32)).astype(BF16)


def station_at(place):
    inside = place & 127
    return ((inside >> 2) << 4) + ((place >> 7) << 2) + (inside & 3)


def packed(state):
    out = state[0:4, :]
    for a in range(1, 4):
        out = out + pltpu.roll(state, 32 * a, 1)[4 * a : 4 * a + 4, :]
    return out


def unpacked(tile):
    rows = [tile] + [pltpu.roll(tile, LANES - 32 * a, 1) for a in range(1, 4)]
    both = jnp.concatenate(rows, axis=0)
    return jnp.where(iota(both.shape, 1) < 2 * DIRS, both, 0.0)


def model_kernel(rows_ref, lmn_ref, flux_ref, map_ref, order_ref, model_ref, gains_ref, own_ref, table_ref, sky_ref, part_ref):
    first = lax.axis_index("stcol") * OWN
    scale = 1.0 + 0.5 * lax.axis_index("freq").astype(F32) / CHANNELS
    pieces = split3(rows_ref[...])
    place = station_at(iota((STATIONS, STATIONS), 0))
    moved = chosen(pieces, as_table(place == iota((STATIONS, STATIONS), 1)))
    gains_ref[...] = moved[0 : 2 * DIRS, :]
    table_ref[...] = as_table(place == order_ref[...])
    mine = as_table(iota((OWN, STATIONS), 1) == iota((OWN, STATIONS), 0) + first)
    own = sum(dot_nt(mine, piece) for piece in pieces[::-1])
    own = jnp.concatenate([own, jnp.zeros((OWN, LANES - own.shape[1]), F32)], axis=1)
    own_ref[...] = jnp.where(iota(own.shape, 1) < 2 * DIRS, own, 0.0)
    count = DIRS * SRC
    member = map_ref[...] == iota((DIRS, count), 0)
    member_f = jnp.where(member, 1.0, 0.0)
    blocks = count // LANES
    stacked = jnp.concatenate([member_f[:, b * LANES : (b + 1) * LANES] for b in range(blocks)], axis=0)
    ahead = as_table(iota((LANES, LANES), 0) <= iota((LANES, LANES), 1))
    running = dot(stacked.astype(BF16), ahead)
    carried = jnp.zeros((DIRS, 1), F32)
    ranks = []
    for b in range(blocks):
        here = running[b * DIRS : (b + 1) * DIRS, :] + carried
        ranks.append(jnp.sum(here * member_f[:, b * LANES : (b + 1) * LANES], axis=0, keepdims=True))
        carried = here[:, LANES - 1 : LANES]
    rank = jnp.concatenate(ranks, axis=1) - 1.0
    slots = as_table(iota((SRC, count), 0) == rank.astype(jnp.int32))
    values = [lmn_ref[0:1, :], lmn_ref[1:2, :], lmn_ref[2:3, :], flux_ref[...]]
    pieces = [[], [], []]
    for value in values:
        for s, piece in enumerate(split3(value)):
            pieces[s].append(piece.astype(F32) * member_f)
    pieces = [jnp.concatenate(p, axis=0).astype(BF16) for p in pieces]
    along = chosen(pieces, slots)
    down = dot_nt(slots, pieces[2]) + dot_nt(slots, pieces[1]) + dot_nt(slots, pieces[0])
    sky_ref[...] = jnp.concatenate([along, along], axis=1)
    part_ref[...] = down
    xyz = [scale * moved[2 * DIRS + c : 2 * DIRS + c + 1, :] for c in range(3)]
    own_xyz = [scale * own[:, 2 * DIRS + c : 2 * DIRS + c + 1] for c in range(3)]
    kept = station_at(iota((OWN, STATIONS), 1)) != iota((OWN, STATIONS), 0) + first
    half = iota((1, LANES), 1) < SRC
    shift_real = jnp.where(half, 0.0, 0.25)
    shift_imag = jnp.where(half, 0.25, 0.5)
    for k in range(DIRS):
        column = [part_ref[:, c * DIRS + k : c * DIRS + k + 1] for c in range(3)]
        turns = wrapped(xyz[0] * column[0] + xyz[1] * column[1] + xyz[2] * column[2])
        wave = jnp.concatenate([cos_turns(turns), sin_turns(turns)], axis=0)
        wave_high, wave_low = split2(wave)
        row = [sky_ref[c * DIRS + k : c * DIRS + k + 1, :] for c in range(4)]
        turns = wrapped(own_xyz[0] * row[0] + own_xyz[1] * row[1] + own_xyz[2] * row[2])
        near = jnp.concatenate([cos_turns(wrapped(turns - shift_real)), cos_turns(wrapped(turns - shift_imag))], axis=0)
        near_high, near_low = split2(near * row[3])
        model = dot(near_high, wave_low) + dot(near_low, wave_high) + dot(near_high, wave_high)
        model_ref[k, 0:OWN, :] = jnp.where(kept, model[0:OWN, :], 0.0)
        model_ref[k, OWN : 2 * OWN, :] = jnp.where(kept, model[OWN:, :], 0.0)


def one_pass(model_ref, vis_ref, gains, own, anchor, penalty, along_ref):
    pred_real = jnp.zeros((OWN, STATIONS), F32)
    pred_imag = jnp.zeros((OWN, STATIONS), F32)
    for k in range(DIRS):
        model_real = model_ref[k, 0:OWN, :]
        model_imag = model_ref[k, OWN : 2 * OWN, :]
        col_real = gains[k : k + 1, :]
        col_imag = gains[DIRS + k : DIRS + k + 1, :]
        along_real = model_real * col_real + model_imag * col_imag
        along_imag = model_imag * col_real - model_real * col_imag
        along_ref[k, 0:OWN, :] = along_real
        along_ref[k, OWN : 2 * OWN, :] = along_imag
        row_real = own[:, k : k + 1]
        row_imag = own[:, DIRS + k : DIRS + k + 1]
        pred_real = pred_real + (row_real * along_real - row_imag * along_imag)
        pred_imag = pred_imag + (row_real * along_imag + row_imag * along_real)
    resid_real = vis_ref[0:OWN, :] - pred_real
    resid_imag = vis_ref[OWN : 2 * OWN, :] - pred_imag
    lane = iota((OWN, LANES), 1)
    numer = jnp.zeros((OWN, LANES), F32)
    denom = jnp.zeros((OWN, LANES), F32)
    for k in range(DIRS):
        along_real = along_ref[k, 0:OWN, :]
        along_imag = along_ref[k, OWN : 2 * OWN, :]
        num_real = jnp.sum(resid_real * along_real + resid_imag * along_imag, axis=1, keepdims=True)
        num_imag = jnp.sum(resid_imag * along_real - resid_real * along_imag, axis=1, keepdims=True)
        den = jnp.sum(along_real * along_real + along_imag * along_imag, axis=1, keepdims=True)
        numer = jnp.where(lane == k, num_real, jnp.where(lane == DIRS + k, num_imag, numer))
        denom = jnp.where((lane == k) | (lane == DIRS + k), den, denom)
    fresh = (numer + own * denom + penalty * anchor) / (denom + penalty)
    return jnp.where(lane < 2 * DIRS, 0.5 * (own + fresh), 0.0)


def gathered_gains(tiles_ref):
    turned = jnp.transpose(tiles_ref[...])
    return jnp.concatenate([turned[32 * a : 32 * a + 32, :] for a in range(4)], axis=1)


def channel_fit(tiles_ref):
    weights = channel_weights(lax.axis_index("freq"))
    total = weights[0] * tiles_ref[0]
    for f in range(1, CHANNELS):
        total = total + weights[f] * tiles_ref[f]
    return unpacked(total)


def first_kernel(model_ref, tiles_ref, table_ref, gains_ref, own_ref, penalty_ref, vis_ref, state_ref, send_ref, along_ref):
    pieces = split3(gathered_gains(tiles_ref))
    vis_ref[...] = chosen(pieces, table_ref[...])
    own = own_ref[...]
    fresh = one_pass(model_ref, vis_ref, gains_ref[...], own, own, penalty_ref[...], along_ref)
    state_ref[...] = fresh
    send_ref[...] = packed(fresh)


def second_kernel(model_ref, vis_ref, tiles_ref, own_ref, anchor_ref, penalty_ref, state_ref, send_ref, along_ref):
    fresh = one_pass(model_ref, vis_ref, gathered_gains(tiles_ref), own_ref[...], anchor_ref[...], penalty_ref[...], along_ref)
    state_ref[...] = fresh
    send_ref[...] = packed(fresh)


def third_kernel(model_ref, vis_ref, tiles_ref, fit_ref, own_ref, penalty_ref, state_ref, anchor_ref, dual_ref, send_ref, along_ref):
    own = own_ref[...]
    cons = channel_fit(fit_ref)
    dual = own - cons
    anchor = cons - dual
    fresh = one_pass(model_ref, vis_ref, gathered_gains(tiles_ref), own, anchor, penalty_ref[...], along_ref)
    state_ref[...] = fresh
    anchor_ref[...] = anchor
    dual_ref[...] = dual
    send_ref[...] = packed(fresh)


def by_direction(state):
    filled = jnp.concatenate([state, jnp.zeros((LANES - OWN, LANES), F32)], axis=0)
    return jnp.transpose(filled)[0 : 2 * DIRS, 0:OWN]


def fourth_kernel(model_ref, vis_ref, tiles_ref, own_ref, anchor_ref, dual_ref, penalty_ref, out_ref, send_ref, along_ref):
    fresh = one_pass(model_ref, vis_ref, gathered_gains(tiles_ref), own_ref[...], anchor_ref[...], penalty_ref[...], along_ref)
    out_ref[...] = by_direction(fresh)
    send_ref[...] = packed(fresh + dual_ref[...])


def last_kernel(fit_ref, out_ref):
    out_ref[...] = by_direction(channel_fit(fit_ref))


def called(kernel, outs, scratch=(), name=None):
    return pl.pallas_call(
        kernel,
        out_shape=[jax.ShapeDtypeStruct(*o) for o in outs],
        scratch_shapes=list(scratch),
        compiler_params=pltpu.CompilerParams(vmem_limit_bytes=48 * 1024 * 1024),
        name=name,
    )


def exchanged(tile, axis):
    count = lax.axis_size(axis)
    tiles = lax.all_to_all(jnp.broadcast_to(tile, (count, *tile.shape)), axis, 0, 0, tiled=True)
    return tiles


def on_device(visibilities, positions, source_lmn, source_flux, cluster_map, station_order, penalty, offsets):
    tiles = visibilities.reshape(2, 4, 4, GROUP, OWN)
    tiles = tiles.transpose(3, 2, 1, 0, 4).reshape(GROUP, 4, LANES)
    tiles = lax.all_to_all(tiles, "stcol", 0, 0, tiled=True).reshape(LANES, LANES)
    order = station_order.reshape(GROUP, 4, 4).transpose(1, 0, 2).reshape(1, STATIONS)
    start = offsets.reshape(2, DIRS, STATIONS)
    rows = jnp.concatenate(
        [1.0 + start[0], start[1], positions.reshape(3, STATIONS), jnp.zeros((5, STATIONS), F32)], axis=0
    )
    pen = jnp.concatenate([penalty, penalty, jnp.ones((LANES - 2 * DIRS,), F32)]).reshape(1, LANES)
    model_out = ((DIRS, 2 * OWN, STATIONS), F32)
    state_out = ((OWN, LANES), F32)
    send_out = ((4, LANES), F32)
    flat_out = ((2 * DIRS, OWN), F32)
    along = pltpu.VMEM((DIRS, 2 * OWN, STATIONS), F32)
    model, gains, own, table = called(
        model_kernel,
        [model_out, ((2 * DIRS, STATIONS), F32), state_out, ((STATIONS, STATIONS), BF16)],
        [pltpu.VMEM((4 * DIRS, 2 * SRC), F32), pltpu.VMEM((SRC, 4 * DIRS), F32)],
        name="models",
    )(rows, source_lmn, source_flux.reshape(1, -1), cluster_map.reshape(1, -1), order)
    vis, state, send = called(
        first_kernel, [((2 * OWN, STATIONS), F32), state_out, send_out], [along], name="pass_one"
    )(model, tiles, table, gains, own, pen)
    got = exchanged(send, "stcol").reshape(LANES, LANES)
    state, send = called(second_kernel, [state_out, send_out], [along], name="pass_two")(
        model, vis, got, state, own, pen
    )
    got = exchanged(send, "stcol").reshape(LANES, LANES)
    fit = exchanged(send, "freq")
    state, anchor, dual, send = called(
        third_kernel, [state_out, state_out, state_out, send_out], [along], name="pass_three"
    )(model, vis, got, fit, state, pen)
    got = exchanged(send, "stcol").reshape(LANES, LANES)
    out, send = called(fourth_kernel, [flat_out, send_out], [along], name="pass_four")(
        model, vis, got, state, anchor, dual, pen
    )
    fit = exchanged(send, "freq")
    (cons,) = called(last_kernel, [flat_out], name="consensus")(fit)
    shape = (2, 1, DIRS, OWN)
    return out.reshape(shape), cons.reshape(shape)


def solution(mesh):
    in_specs = (
        P(None, "freq", "stcol", None, None),
        P(),
        P(),
        P(),
        P(),
        P(),
        P(),
        P(None, "freq", None, None),
    )
    out_specs = (P(None, "freq", None, "stcol"), P(None, "freq", None, "stcol"))
    return jax.shard_map(
        on_device, mesh=mesh, in_specs=in_specs, out_specs=out_specs, check_vma=False
    )
```

time: 293 us -> 91.3 us (0.31)
  matrix products: 85.7 us -> 0 us
  local copies, waits for them, and re-layouts: 45.9 us -> 3.37 us
  other arithmetic: 39 us -> 1.16 us
  waiting for transfers between devices: 22 us -> 1.15 us
  starting transfers between devices: 23 us -> 12 us
  Pallas kernels: 0 us -> 9.99 us
  blocking collectives: 69.8 us -> 62.3 us
  between operations: 4.85 us -> 0.78 us
    dot_general x68 -> x0, matrix products: 85.7 us -> none  [the longest x64 83.9 us: contract(): jnp.einsum('ctps,ctjs->cjtp', row_part, column_part, precision=HIGHEST)]
    gather x40 -> x0, local copies, waits for them, and re-layouts: 28.2 us -> none  [the longest x16 9.22 us: model_block(): column_sin = jnp.take(sine_part, column_ids, axis=2)]
    all_to_all x4 -> x1, waiting for transfers between devices: 22 us -> 1.15 us  [on_device(): lax.all_to_all(tiles, 'stcol', 0, 0, tiled=True).reshape(LANES, LANES)]
    another operation x20 -> x0, other arithmetic: 16.6 us -> none  [the longest x16 16.5 us: model_block(): column_sin = jnp.take(sine_part, column_ids, axis=2)]
    all_to_all x4 -> x1, starting transfers between devices: 23 us -> 12 us  [on_device(): lax.all_to_all(tiles, 'stcol', 0, 0, tiled=True).reshape(LANES, LANES)]
    pallas_call x0 -> x6, Pallas kernels: none -> 9.99 us  [the longest x1 5.27 us: on_device(): called(model_kernel, [model_out, ((2 * DIRS, STATIONS), F32), state_out,...]
    all_to_all x5, blocking collectives: 69.8 us -> 62.3 us  [exchanged(): lax.all_to_all(jnp.broadcast_to(tile, (count, *tile.shape)), axis, 0, 0,...]
    unnamed x40 -> x15, local copies, waits for them, and re-layouts: 9.25 us -> 1.85 us
  transfers between devices with their start and end apart: 4 -> 1, of which waited for: 4 -> 1; matrix products, arithmetic and copies ran while one was open for 2% -> 1% of each run, Pallas kernels for 0% -> 6%
where the time goes in v1:
time: 91.3 us; the launch traced here: 90.8 us
  blocking collectives  62.3 us (68%)
  starting transfers between devices  12 us (13%)
  Pallas kernels  9.99 us (11%)
  local copies, waits for them, and re-layouts  3.37 us (4%)
  other arithmetic  1.16 us (1%)
  waiting for transfers between devices  1.15 us (1%)
    all_to_all x5, blocking collectives, exchanged(): lax.all_to_all(jnp.broadcast_to(tile, (count, *tile.shape)), axis, 0, 0,...  62.3 us
    all_to_all x1, starting transfers between devices, on_device(): lax.all_to_all(tiles, 'stcol', 0, 0, tiled=True).reshape(LANES, LANES)  12 us
    pallas_call x1, Pallas kernels, on_device(): called(model_kernel, [model_out, ((2 * DIRS, STATIONS), F32), state_out,...  5.27 us
    unnamed x15, local copies, waits for them, and re-layouts  1.85 us
  transfers between devices with their start and end apart: 1, of which 1 were waited for; matrix products, arithmetic and copies ran while one was open for 1% of the time, Pallas kernels for 6%

profile of v1, /device:TPU:1, one launch (start us, length us, event | category | flops | bytes accessed | tf_op | source)
XLA Modules:
  0.0 90.8 jit_solution(16254383142798707231)
XLA Ops:
  0.6 1.0 %reduce = f32[2,16,512]{2,1,0:T(8,128)S(1)} reduce(f32[2,1,16,1,512]{4,3,2,1,0:T(1,128)} %param.8, f32[]{:T(128)} %constant.7), dimensions={1,3}, to_apply=%param.8.reduce_sub_computation | reduce | bytes 131076 | tf_op args[0]
  1.6 0.2 reshape.58
  1.8 0.2 copy.19
  2.0 0.7 copy.20
  2.8 12.0 %all-to-all-start = ((f32[32,4,128]{2,1,0:T(4,128)}), f32[32,4,128]{2,1,0:T(4,128)S(1)}, u32[]{:S(2)}, u32[]{:S(2)}) async-start(f32[32,4,128]{2,1,0:T(4,128)} %copy.20), calls=%async_computation | async-start | bytes 131072 | tf_op jit(solution)/shard_map/all_to_all | solution.py:304
  14.9 0.1 maximum_maximum_fusion.rows_ref
  15.0 0.6 copy-done.5
  15.6 0.1 reshape.56
  15.8 0.1 reshape.57.order_ref
  15.9 0.6 copy-done
  16.5 5.3 %models.1 = (f32[16,32,512]{2,1,0:T(8,128)S(1)}, f32[32,512]{1,0:T(8,128)S(1)}, f32[16,128]{1,0:T(8,128)S(1)}, bf16[512,512]{1,0:T(8,128)(2,1)S(1)}) custom-call(f32[40,512]{1,0:T(8,128)S(1)} %maximum_maximum_fusion.rows_ref, f32[3,1024]{1,0:T(4,128)S(1)} %copy-done, f32[1,1024]{1,0:T(1,128)S(1)} %bitcast.28, s32[1,1024]{1,0:T(1,128)S(1)} %bitcast.29, ...), custom_call_target="tpu_custom_call" | custom-call | tf_op jit(solution)/shard_map/models/pallas_call | solution.py:316
  21.8 0.6 copy-done.6
  22.4 0.1 maximum_bitcast_fusion.penalty_ref
  22.5 1.2 %all-to-all-done = f32[32,4,128]{2,1,0:T(4,128)S(1)} async-done(((f32[32,4,128]{2,1,0:T(4,128)}), f32[32,4,128]{2,1,0:T(4,128)S(1)}, u32[]{:S(2)}, u32[]{:S(2)}) %all-to-all-start) | async-done | bytes 65568 | tf_op jit(solution)/shard_map/all_to_all | solution.py:304
  23.6 1.0 %pass_one.1 = (f32[32,512]{1,0:T(8,128)S(1)}, f32[16,128]{1,0:T(8,128)S(1)}, f32[4,128]{1,0:T(4,128)S(1)}) custom-call(f32[16,32,512]{2,1,0:T(8,128)S(1)} %get-tuple-element.17.model_ref, f32[128,128]{1,0:T(8,128)S(1)} %bitcast.24, bf16[512,512]{1,0:T(8,128)(2,1)S(1)} %get-tuple-element.18.table_ref, f32[32,512]{1,0:T(8,128)S(1)} %get-tuple-element.19.gains_ref, ...), custom_call_target="tpu_custom_call" | custom-call | tf_op jit(solution)/shard_map/pass_one/pallas_call | solution.py:322
  24.7 16.8 %all_to_all.30 = f32[32,4,128]{2,1,0:T(4,128)S(1)} all-to-all(f32[32,4,128]{2,1,0:T(4,128)S(1)} %broadcast_in_dim.23), channel_id=1, replica_groups=mesh['freq'=8,'stcol'=32] {'stcol'}, dimensions={0} | all-to-all | bytes 131072 | tf_op jit(solution)/shard_map/all_to_all | solution.py:297
  41.5 0.8 pass_two.1
  42.3 11.5 %all_to_all.31.fit_ref = f32[8,4,128]{2,1,0:T(4,128)S(1)} all-to-all(f32[8,4,128]{2,1,0:T(4,128)S(1)} %broadcast_in_dim.25), channel_id=1, replica_groups=mesh['freq'=8,'stcol'=32] {'freq'}, dimensions={0} | all-to-all | bytes 32768 | tf_op jit(solution)/shard_map/all_to_all | solution.py:297
  53.8 11.8 %all_to_all.32 = f32[32,4,128]{2,1,0:T(4,128)S(1)} all-to-all(f32[32,4,128]{2,1,0:T(4,128)S(1)} %broadcast_in_dim.24), channel_id=1, replica_groups=mesh['freq'=8,'stcol'=32] {'stcol'}, dimensions={0} | all-to-all | bytes 131072 | tf_op jit(solution)/shard_map/all_to_all | solution.py:297
  65.6 0.8 pass_three.1
  66.4 12.0 %all_to_all.33 = f32[32,4,128]{2,1,0:T(4,128)S(1)} all-to-all(f32[32,4,128]{2,1,0:T(4,128)S(1)} %broadcast_in_dim.26), channel_id=1, replica_groups=mesh['freq'=8,'stcol'=32] {'stcol'}, dimensions={0} | all-to-all | bytes 131072 | tf_op jit(solution)/shard_map/all_to_all | solution.py:297
  78.4 1.4 %pass_four.1 = (f32[32,16]{1,0:T(8,128)}, f32[4,128]{1,0:T(4,128)S(1)}) custom-call(f32[16,32,512]{2,1,0:T(8,128)S(1)} %get-tuple-element.17.model_ref, f32[32,512]{1,0:T(8,128)S(1)} %get-tuple-element.21.vis_ref, f32[128,128]{1,0:T(8,128)S(1)} %bitcast.25, f32[16,128]{1,0:T(8,128)S(1)} %get-tuple-element.27.own_ref, ...), custom_call_target="tpu_custom_call" | custom-call | tf_op jit(solution)/shard_map/pass_four/pallas_call | solution.py:335
  79.8 10.2 %all_to_all.34.fit_ref = f32[8,4,128]{2,1,0:T(4,128)S(1)} all-to-all(f32[8,4,128]{2,1,0:T(4,128)S(1)} %broadcast_in_dim.27), channel_id=1, replica_groups=mesh['freq'=8,'stcol'=32] {'freq'}, dimensions={0} | all-to-all | bytes 32768 | tf_op jit(solution)/shard_map/all_to_all | solution.py:297
  90.0 0.8 consensus.1
  (22 shorter events, 0.2 us)
Async XLA Ops:
  2.8 12.0 %copy-start.4 = (f32[3,1,512]{2,1,0:T(1,128)S(1)}, f32[3,1,512]{2,1,0:T(1,128)}, u32[]{:S(2)}) copy-start(f32[3,1,512]{2,1,0:T(1,128)} %param.9) | copy-start | bytes 18436
  2.8 12.0 %copy-start.3 = (f32[2,1,16,512]{3,2,1,0:T(8,128)S(1)}, f32[2,1,16,512]{3,2,1,0:T(8,128)}, u32[]{:S(2)}) copy-start(f32[2,1,16,512]{3,2,1,0:T(8,128)} %param.15) | copy-start | bytes 196612
  2.8 20.9 %all-to-all-start = ((f32[32,4,128]{2,1,0:T(4,128)}), f32[32,4,128]{2,1,0:T(4,128)S(1)}, u32[]{:S(2)}, u32[]{:S(2)}) async-start(f32[32,4,128]{2,1,0:T(4,128)} %copy.20), calls=%async_computation | async-start | bytes 131072 | tf_op jit(solution)/shard_map/all_to_all | solution.py:304
  14.9 0.7 copy-start.5
  15.8 0.7 copy-start
  15.8 0.7 copy-start.1
  15.8 0.7 copy-start.2
  21.8 0.7 copy-start.6

commit v2 on v1

v2 whole, which is shorter than its diff:
```python
import math

import jax
import jax.numpy as jnp
import numpy as np
from jax import lax
from jax.experimental import pallas as pl
from jax.experimental.pallas import tpu as pltpu
from jax.sharding import PartitionSpec as P

STATIONS = 512
DIRS = 16
SRC = 64
CHANNELS = 8
OWN = 16
REPS = 2
ROWS = REPS * OWN
MEMBERS = STATIONS // ROWS
LANES = 128
F32 = jnp.float32
BF16 = jnp.bfloat16

COS_TERMS = None
SIN_TERMS = None


def fit_terms():
    nodes = np.cos(np.pi * (np.arange(400) + 0.5) / 400)
    u = 0.125 * (nodes + 1.0)
    r = np.sqrt(u)
    cheb = np.polynomial.chebyshev
    poly = np.polynomial.polynomial

    def terms(values, degree):
        series = cheb.cheb2poly(cheb.chebfit(nodes, values, degree))
        out = np.zeros(1)
        for c in series[::-1]:
            out = poly.polyadd(poly.polymul(out, [-1.0, 8.0]), [c])
        return [float(np.float32(c)) for c in out[: degree + 1]]

    return terms(np.cos(2 * np.pi * r), 7), terms(np.sin(2 * np.pi * r) / r, 6)


COS_TERMS, SIN_TERMS = fit_terms()


def basis_table():
    centre = (np.arange(CHANNELS) - 0.5 * (CHANNELS - 1)) / CHANNELS
    columns = [np.ones_like(centre), centre, centre * centre]
    finished = []
    for column in columns:
        for before in finished:
            column = column - np.sum(column * before) * before
        finished.append(column / np.sqrt(np.sum(column * column)))
    return np.stack(finished, axis=1)


BASIS = basis_table()


def basis_row(channel):
    centre = (np.arange(CHANNELS) - 0.5 * (CHANNELS - 1)) / CHANNELS
    square = centre * centre
    flat = BASIS[:, 0]
    lift = float(np.sum(square * flat))
    norm1 = float(np.sqrt(np.sum(centre * centre)))
    norm2 = float(np.sqrt(np.sum((square - lift * flat) ** 2)))
    x = (channel.astype(F32) - 0.5 * (CHANNELS - 1)) * (1.0 / CHANNELS)
    return (float(flat[0]), x * (1.0 / norm1), (x * x - lift * float(flat[0])) * (1.0 / norm2))


def channel_weights(channel):
    row = basis_row(channel)
    return [sum(row[j] * float(BASIS[f, j]) for j in range(3)) for f in range(CHANNELS)]


def channel_weight(channel, source):
    return sum(a * b for a, b in zip(basis_row(channel), basis_row(source)))


def horner(u, terms):
    out = jnp.full_like(u, terms[-1])
    for c in terms[-2::-1]:
        out = out * u + c
    return out


def wrapped(turns):
    return turns - jnp.round(turns)


def cos_turns(r):
    return horner(r * r, COS_TERMS)


def sin_turns(r):
    return r * horner(r * r, SIN_TERMS)


def split2(x):
    high = x.astype(BF16)
    return high, (x - high.astype(F32)).astype(BF16)


def split3(x):
    high = x.astype(BF16)
    rest = x - high.astype(F32)
    mid = rest.astype(BF16)
    return high, mid, (rest - mid.astype(F32)).astype(BF16)


def dot(a, b):
    return lax.dot_general(a, b, (((1,), (0,)), ((), ())), preferred_element_type=F32)


def dot_nt(a, b):
    return lax.dot_general(a, b, (((1,), (1,)), ((), ())), preferred_element_type=F32)


def chosen(pieces, table):
    return dot_nt(pieces[2], table) + dot_nt(pieces[1], table) + dot_nt(pieces[0], table)


def iota(shape, dim):
    return lax.broadcasted_iota(jnp.int32, shape, dim)


def as_table(cond):
    return jnp.where(cond, jnp.ones(cond.shape, F32), jnp.zeros(cond.shape, F32)).astype(BF16)


def station_at(place):
    member = (place >> 3) & 15
    return ((member >> 2) << 7) + ((place >> 8) << 6) + ((member & 3) << 4) + (((place >> 7) & 1) << 3) + (place & 7)


def row_station(shape, dim, device):
    row = iota(shape, dim)
    return ((row >> 4) << 6) + (row & 15) + ((device >> 3) << 7) + ((device & 3) << 4)


def rep_of(device):
    return (device & 7) >> 2


def packed(state):
    n = state.shape[0] // 4
    out = state[0:n, :]
    for a in range(1, 4):
        out = out + pltpu.roll(state, 32 * a, 1)[n * a : n * a + n, :]
    return out


def unpacked(tile):
    rows = [tile] + [pltpu.roll(tile, LANES - 32 * a, 1) for a in range(1, 4)]
    both = jnp.concatenate(rows, axis=0)
    return jnp.where(iota(both.shape, 1) < 2 * DIRS, both, 0.0)


def turn_kernel(vis_hbm, tiles_ref, vis_ref, sem):
    copy = pltpu.make_async_copy(vis_hbm, vis_ref, sem)
    copy.start()
    copy.wait()
    lane = iota((8, LANES), 1)
    for x in range(4):
        parts = [vis_ref[r * 8 : (r + 1) * 8, 0, x * LANES : (x + 1) * LANES] for r in range(4)]
        for b in range(4):
            tile = jnp.zeros((8, LANES), F32)
            for half in range(2):
                for r in range(2):
                    for a in range(REPS):
                        to = half * 64 + r * ROWS + a * OWN
                        moved = pltpu.roll(parts[2 * r + half], (to - (64 * a + 16 * b)) % LANES, 1)
                        tile = jnp.where((lane >> 4) == (to >> 4), moved, tile)
            for a in range(REPS):
                tiles_ref[x * 8 + 4 * a + b] = tile


def products(model_ref, gains_ref, start, k):
    half = model_ref.shape[1] // 2
    model_real = model_ref[k, pl.ds(start, OWN), :]
    model_imag = model_ref[k, pl.ds(start + half, OWN), :]
    col_real = gains_ref[k : k + 1, :]
    col_imag = gains_ref[DIRS + k : DIRS + k + 1, :]
    return model_real * col_real + model_imag * col_imag, model_imag * col_real - model_real * col_imag


def predict(model_ref, gains_ref, own, start, along_ref):
    pred_real = jnp.zeros((OWN, STATIONS), F32)
    pred_imag = jnp.zeros((OWN, STATIONS), F32)
    lane = iota((OWN, LANES), 1)
    denom = jnp.zeros((OWN, LANES), F32)
    for k in range(DIRS):
        along_real, along_imag = products(model_ref, gains_ref, start, k)
        if along_ref is not None:
            along_ref[k, 0:OWN, :] = along_real
            along_ref[k, OWN : 2 * OWN, :] = along_imag
        row_real = own[:, k : k + 1]
        row_imag = own[:, DIRS + k : DIRS + k + 1]
        pred_real = pred_real + (row_real * along_real - row_imag * along_imag)
        pred_imag = pred_imag + (row_real * along_imag + row_imag * along_real)
        den = jnp.sum(along_real * along_real + along_imag * along_imag, axis=1, keepdims=True)
        denom = jnp.where((lane == k) | (lane == DIRS + k), den, denom)
    return pred_real, pred_imag, denom


def correlate(resid_real, resid_imag, along):
    lane = iota((OWN, LANES), 1)
    numer = jnp.zeros((OWN, LANES), F32)
    for k in range(DIRS):
        along_real, along_imag = along(k)
        num_real = jnp.sum(resid_real * along_real + resid_imag * along_imag, axis=1, keepdims=True)
        num_imag = jnp.sum(resid_imag * along_real - resid_real * along_imag, axis=1, keepdims=True)
        numer = jnp.where(lane == k, num_real, jnp.where(lane == DIRS + k, num_imag, numer))
    return numer


def row_sums(model_ref, vis_ref, gains_ref, own, start, along_ref):
    pred_real, pred_imag, denom = predict(model_ref, gains_ref, own, start, along_ref)
    resid_real = vis_ref[pl.ds(start, OWN), :] - pred_real
    resid_imag = vis_ref[pl.ds(start + ROWS, OWN), :] - pred_imag
    numer = correlate(resid_real, resid_imag, lambda k: (along_ref[k, 0:OWN, :], along_ref[k, OWN : 2 * OWN, :]))
    return numer, denom


def updated(numer, denom, own, anchor, penalty):
    fresh = (numer + own * denom + penalty * anchor) / (denom + penalty)
    return jnp.where(iota(own.shape, 1) < 2 * DIRS, 0.5 * (own + fresh), 0.0)


def model_kernel(
    offs_hbm, place_hbm, lmn_hbm, flux_hbm, map_hbm, order_ref, penalty_hbm,
    model_ref, own_ref, table_ref, gains_ref, pred_ref, den_ref, weight_ref,
    offs_ref, xyz_ref, lmn_ref, flux_ref, map_ref, penalty_ref, sky_ref, part_ref, sems,
):
    pairs = [
        (map_hbm, map_ref), (lmn_hbm, lmn_ref), (flux_hbm, flux_ref),
        (offs_hbm, offs_ref), (place_hbm, xyz_ref), (penalty_hbm, penalty_ref),
    ]
    copies = [pltpu.make_async_copy(a, b, sems.at[n]) for n, (a, b) in enumerate(pairs)]
    for copy in copies:
        copy.start()
    device = lax.axis_index("stcol")
    scale = 1.0 + 0.5 * lax.axis_index("freq").astype(F32) / CHANNELS
    for copy in copies:
        copy.wait()
    lane = iota((1, LANES), 1)
    weight = jnp.ones((1, LANES), F32)
    for k in range(DIRS):
        weight = jnp.where((lane == k) | (lane == DIRS + k), penalty_ref[0, k], weight)
    weight_ref[...] = weight
    offs = offs_ref[...]
    rows = [1.0 + offs[0:DIRS, :], offs[DIRS : 2 * DIRS, :]] + [xyz_ref[c] for c in range(3)]
    pieces = split3(jnp.concatenate(rows + [jnp.zeros((5, STATIONS), F32)], axis=0))
    place = station_at(iota((STATIONS, STATIONS), 0))
    moved = chosen(pieces, as_table(place == iota((STATIONS, STATIONS), 1)))
    gains_ref[...] = moved[0 : 2 * DIRS, :]
    table_ref[...] = as_table(place == order_ref[...])
    mine = as_table(iota((ROWS, STATIONS), 1) == row_station((ROWS, STATIONS), 0, device))
    own = sum(dot_nt(mine, piece) for piece in pieces[::-1])
    own = jnp.concatenate([own, jnp.zeros((ROWS, LANES - own.shape[1]), F32)], axis=1)
    own_xyz = [scale * own[:, 2 * DIRS + c : 2 * DIRS + c + 1] for c in range(3)]
    own_ref[...] = jnp.where(iota(own.shape, 1) < 2 * DIRS, own, 0.0)
    count = DIRS * SRC
    member = map_ref[...] == iota((DIRS, count), 0)
    member_f = jnp.where(member, 1.0, 0.0)
    blocks = count // LANES
    stacked = jnp.concatenate([member_f[:, b * LANES : (b + 1) * LANES] for b in range(blocks)], axis=0)
    ahead = as_table(iota((LANES, LANES), 0) <= iota((LANES, LANES), 1))
    running = dot(stacked.astype(BF16), ahead)
    carried = jnp.zeros((DIRS, 1), F32)
    ranks = []
    for b in range(blocks):
        here = running[b * DIRS : (b + 1) * DIRS, :] + carried
        ranks.append(jnp.sum(here * member_f[:, b * LANES : (b + 1) * LANES], axis=0, keepdims=True))
        carried = here[:, LANES - 1 : LANES]
    rank = jnp.concatenate(ranks, axis=1) - 1.0
    slots = as_table(iota((SRC, count), 0) == rank.astype(jnp.int32))
    values = [lmn_ref[0:1, :], lmn_ref[1:2, :], lmn_ref[2:3, :], flux_ref[...]]
    pieces = [[], [], []]
    for value in values:
        for s, piece in enumerate(split3(value)):
            pieces[s].append(piece.astype(F32) * member_f)
    pieces = [jnp.concatenate(p, axis=0).astype(BF16) for p in pieces]
    along = chosen(pieces, slots)
    down = dot_nt(slots, pieces[2]) + dot_nt(slots, pieces[1]) + dot_nt(slots, pieces[0])
    sky_ref[...] = jnp.concatenate([along, along], axis=1)
    part_ref[...] = down
    xyz = [scale * moved[2 * DIRS + c : 2 * DIRS + c + 1, :] for c in range(3)]
    kept = station_at(iota((ROWS, STATIONS), 1)) != row_station((ROWS, STATIONS), 0, device)
    half = iota((1, LANES), 1) < SRC
    shift_real = jnp.where(half, 0.0, 0.25)
    shift_imag = jnp.where(half, 0.25, 0.5)
    for k in range(DIRS):
        column = [part_ref[:, c * DIRS + k : c * DIRS + k + 1] for c in range(3)]
        turns = wrapped(xyz[0] * column[0] + xyz[1] * column[1] + xyz[2] * column[2])
        wave = jnp.concatenate([cos_turns(turns), sin_turns(turns)], axis=0)
        wave_high, wave_low = split2(wave)
        row = [sky_ref[c * DIRS + k : c * DIRS + k + 1, :] for c in range(4)]
        turns = wrapped(own_xyz[0] * row[0] + own_xyz[1] * row[1] + own_xyz[2] * row[2])
        near = jnp.concatenate([cos_turns(wrapped(turns - shift_real)), cos_turns(wrapped(turns - shift_imag))], axis=0)
        near_high, near_low = split2(near * row[3])
        model = dot(near_high, wave_low) + dot(near_low, wave_high) + dot(near_high, wave_high)
        model_ref[k, 0:ROWS, :] = jnp.where(kept, model[0:ROWS, :], 0.0)
        model_ref[k, ROWS : 2 * ROWS, :] = jnp.where(kept, model[ROWS:, :], 0.0)
    for a in range(REPS):
        rows = slice(a * OWN, (a + 1) * OWN)
        pred_real, pred_imag, denom = predict(model_ref, gains_ref, own_ref[rows, :], a * OWN, None)
        pred_ref[rows, :] = pred_real
        pred_ref[ROWS + a * OWN : ROWS + (a + 1) * OWN, :] = pred_imag
        den_ref[rows, :] = denom


def gathered_gains(tiles_ref):
    turned = jnp.transpose(tiles_ref[...])
    return jnp.concatenate([turned[32 * a : 32 * a + 32, :] for a in range(4)], axis=1)


def channel_fit(tiles_ref):
    weights = channel_weights(lax.axis_index("freq"))
    total = weights[0] * tiles_ref[0]
    for f in range(1, CHANNELS):
        total = total + weights[f] * tiles_ref[f]
    return total


def sums(model_ref, vis_ref, tiles_ref, own_ref, numer_ref, den_ref, along_ref, gains_ref):
    gains_ref[...] = gathered_gains(tiles_ref)
    for a in range(REPS):
        rows = slice(a * OWN, (a + 1) * OWN)
        numer, denom = row_sums(model_ref, vis_ref, gains_ref, own_ref[rows, :], a * OWN, along_ref)
        numer_ref[rows, :] = numer
        den_ref[rows, :] = denom


def first_kernel(tiles_ref, table_ref, model_ref, gains_ref, pred_ref, den_ref, own_ref, penalty_ref, vis_ref, state_ref, send_ref):
    turned = jnp.transpose(tiles_ref[...])
    pieces = split3(jnp.concatenate([turned[0 : 2 * ROWS, :], turned[2 * ROWS :, :]], axis=1))
    vis_ref[...] = chosen(pieces, table_ref[...])
    for a in range(REPS):
        rows = slice(a * OWN, (a + 1) * OWN)
        lower = slice(ROWS + a * OWN, ROWS + (a + 1) * OWN)
        resid_real = vis_ref[rows, :] - pred_ref[rows, :]
        resid_imag = vis_ref[lower, :] - pred_ref[lower, :]
        numer = correlate(resid_real, resid_imag, lambda k: products(model_ref, gains_ref, a * OWN, k))
        own = own_ref[rows, :]
        state_ref[rows, :] = updated(numer, den_ref[rows, :], own, own, penalty_ref[...])
    send_ref[...] = packed(state_ref[...])


def second_kernel(
    model_ref, vis_ref, tiles_ref, own_ref, anchor_ref, penalty_ref, state_ref, send_ref, along_ref, gains_ref, den_ref
):
    sums(model_ref, vis_ref, tiles_ref, own_ref, state_ref, den_ref, along_ref, gains_ref)
    state = updated(state_ref[...], den_ref[...], own_ref[...], anchor_ref[...], penalty_ref[...])
    state_ref[...] = state
    send_ref[...] = packed(state)


def anchor_kernel(numer_ref, den_ref, near_ref, far_ref, own_ref, penalty_ref, state_ref, anchor_ref, dual_ref, send_ref):
    own = own_ref[...]
    channel = lax.axis_index("freq")
    total = None
    for d in range(CHANNELS // 2):
        other = (channel - 2 * d) & (CHANNELS - 1)
        for tiles_ref, source in ((near_ref, other), (far_ref, other ^ 1)):
            part = channel_weight(channel, source) * tiles_ref[d]
            total = part if total is None else total + part
    cons = unpacked(total)
    dual = own - cons
    anchor = cons - dual
    state = updated(numer_ref[...], den_ref[...], own, anchor, penalty_ref[...])
    state_ref[...] = state
    send_ref[...] = packed(state)
    anchor_ref[...] = anchor
    dual_ref[...] = dual


def by_direction(state):
    filled = jnp.concatenate([state, jnp.zeros((LANES - OWN, LANES), F32)], axis=0)
    return jnp.transpose(filled)[0 : 2 * DIRS, 0:OWN]


def fourth_kernel(
    model_ref, vis_ref, tiles_ref, own_ref, anchor_ref, dual_ref, penalty_ref, state_ref, send_ref, along_ref, gains_ref
):
    start = pl.multiple_of(rep_of(lax.axis_index("stcol")) * OWN, OWN)
    rows = pl.ds(start, OWN)
    own = own_ref[rows, :]
    gains_ref[...] = gathered_gains(tiles_ref)
    numer, denom = row_sums(model_ref, vis_ref, gains_ref, own, start, along_ref)
    state = updated(numer, denom, own, anchor_ref[rows, :], penalty_ref[...])
    state_ref[...] = state
    send_ref[...] = packed(state + dual_ref[rows, :])


def last_kernel(fit_ref, state_ref, out_ref, cons_ref):
    out_ref[...] = by_direction(state_ref[...])
    cons_ref[...] = by_direction(unpacked(channel_fit(fit_ref)))


def called(kernel, outs, scratch=(), name=None, in_specs=None):
    return pl.pallas_call(
        kernel,
        out_shape=[jax.ShapeDtypeStruct(*o) for o in outs],
        scratch_shapes=[pltpu.VMEM(*o) if isinstance(o, tuple) else o for o in scratch],
        compiler_params=pltpu.CompilerParams(vmem_limit_bytes=32 * 1024 * 1024),
        name=name,
        **({} if in_specs is None else {"in_specs": in_specs}),
    )


def held(x):
    return pltpu.with_memory_space_constraint(x, pltpu.HBM)


def to_all(tile, axis, count, groups=None):
    tiles = jnp.broadcast_to(tile, (count, *tile.shape))
    return lax.all_to_all(tiles, axis, 0, 0, tiled=True, axis_index_groups=groups)


def to_members(tile):
    groups = [[x * 8 + 4 * m + b for x in range(4) for b in range(4)] for m in range(REPS)]
    return to_all(tile, "stcol", MEMBERS, groups).reshape(LANES, LANES)


def on_device(visibilities, positions, source_lmn, source_flux, cluster_map, station_order, penalty, offsets):
    hbm = pl.BlockSpec(memory_space=pltpu.HBM)
    vmem = pl.BlockSpec(memory_space=pltpu.VMEM)
    model_out = ((DIRS, 2 * ROWS, STATIONS), F32)
    along = ((DIRS, 2 * OWN, STATIONS), F32)
    vis_out = ((2 * ROWS, STATIONS), F32)
    state_out = ((ROWS, LANES), F32)
    send_out = ((ROWS // 4, LANES), F32)
    flat_out = ((2 * DIRS, OWN), F32)
    gains_out = ((2 * DIRS, STATIONS), F32)
    (tiles,) = called(
        turn_kernel,
        [((STATIONS // OWN, 8, LANES), F32)],
        [((2 * OWN, 1, STATIONS), F32), pltpu.SemaphoreType.DMA],
        "turn",
        [hbm],
    )(held(visibilities.reshape(2 * OWN, 1, STATIONS)))
    tiles = lax.all_to_all(tiles, "stcol", 0, 0, tiled=True).reshape(STATIONS // 2, LANES)
    order = station_order.reshape(STATIONS // OWN, 2, 8).transpose(1, 0, 2).reshape(1, STATIONS)
    count = DIRS * SRC
    model, own, table, gains, pred, den, pen = called(
        model_kernel,
        [model_out, state_out, ((STATIONS, STATIONS), BF16), gains_out, vis_out, state_out, ((1, LANES), F32)],
        [
            gains_out, ((3, 1, STATIONS), F32), ((3, count), F32), ((1, count), F32), ((1, count), jnp.int32),
            pltpu.SMEM((1, DIRS), F32), ((4 * DIRS, 2 * SRC), F32), ((SRC, 4 * DIRS), F32),
            pltpu.SemaphoreType.DMA((6,)),
        ],
        "models",
        [hbm, hbm, hbm, hbm, hbm, vmem, hbm],
    )(
        held(offsets.reshape(2 * DIRS, STATIONS)), held(positions), held(source_lmn), held(source_flux.reshape(1, count)),
        held(cluster_map.reshape(1, count)), order, held(penalty.reshape(1, DIRS)),
    )
    vis, state, send = called(first_kernel, [vis_out, state_out, send_out], name="pass_one")(
        tiles, table, model, gains, pred, den, own, pen
    )
    got = to_members(send)
    state, send = called(second_kernel, [state_out, send_out], [along, gains_out, state_out], "pass_two")(
        model, vis, got, state, own, pen
    )
    near = [send] + [
        lax.ppermute(send, "freq", [(i, (i + 2 * d) % CHANNELS) for i in range(CHANNELS)]) for d in range(1, CHANNELS // 2)
    ]
    near = jnp.stack(near)
    far = lax.ppermute(near, "freq", [(i, i ^ 1) for i in range(CHANNELS)])
    got = to_members(send)
    numer, den = called(sums, [state_out, state_out], [along, gains_out], "pass_three")(model, vis, got, state)
    state, anchor, dual, send = called(anchor_kernel, [state_out, state_out, state_out, send_out], name="update_three")(
        numer, den, near, far, state, pen
    )
    got = to_members(send)
    state, send = called(fourth_kernel, [((OWN, LANES), F32), ((4, LANES), F32)], [along, gains_out], "pass_four")(
        model, vis, got, state, anchor, dual, pen
    )
    out, cons = called(last_kernel, [flat_out, flat_out], name="consensus")(to_all(send, "freq", CHANNELS), state)
    shape = (2, 1, DIRS, OWN)
    return out.reshape(shape), cons.reshape(shape)


def solution(mesh):
    in_specs = (
        P(None, "freq", "stcol", None, None),
        P(),
        P(),
        P(),
        P(),
        P(),
        P(),
        P(None, "freq", None, None),
    )
    out_specs = (P(None, "freq", None, "stcol"), P(None, "freq", None, "stcol"))
    return jax.shard_map(
        on_device, mesh=mesh, in_specs=in_specs, out_specs=out_specs, check_vma=False
    )
```

time: 91.3 us -> 80.6 us (0.88)
  blocking collectives: 62.3 us -> 35.8 us
  starting transfers between devices: 12 us -> 22.8 us
  Pallas kernels: 9.99 us -> 14.9 us
  waiting for transfers between devices: 1.15 us -> 4.41 us
  local copies, waits for them, and re-layouts: 3.37 us -> 1.53 us
  other arithmetic: 1.16 us -> 0.01 us
    all_to_all x5 -> x3, blocking collectives: 62.3 us -> 35.8 us  [to_all(): lax.all_to_all(tiles, axis, 0, 0, tiled=True, axis_index_groups=groups)]
    ppermute x0 -> x4, starting transfers between devices: none -> 7.46 us  [the longest x3 3.79 us: on_device(): lax.ppermute(send, 'freq', [(i, (i + 2 * d) % CHANNELS) for i in range(CH...]
    pallas_call x6 -> x8, Pallas kernels: 9.99 us -> 14.9 us  [the longest x1 7.06 us: on_device(): called(model_kernel, [model_out, state_out, ((STATIONS, STATIONS), BF16),...]
    all_to_all x1 -> x2, starting transfers between devices: 12 us -> 15.4 us  [the longest x1 11.9 us: on_device(): lax.all_to_all(tiles, 'stcol', 0, 0, tiled=True)]
    all_to_all x1 -> x2, waiting for transfers between devices: 1.15 us -> 4.4 us  [the longest x1 3.21 us: to_all(): lax.all_to_all(tiles, axis, 0, 0, tiled=True, axis_index_groups=groups)]
    unnamed x15 -> x0, local copies, waits for them, and re-layouts: 1.85 us -> none
    unnamed x1 -> x0, other arithmetic: 1 us -> none
  transfers between devices with their start and end apart: 1 -> 6, of which waited for: 1 -> 2; matrix products, arithmetic and copies ran while one was open for 1% -> 2% of each run, Pallas kernels for 6% -> 11%
where the time goes in v2:
time: 80.6 us; the launch traced here: 80.2 us
  blocking collectives  35.8 us (44%)
  starting transfers between devices  22.8 us (28%)
  Pallas kernels  14.9 us (18%)
  waiting for transfers between devices  4.41 us (5%)
  local copies, waits for them, and re-layouts  1.53 us (2%)
    all_to_all x3, blocking collectives, to_all(): lax.all_to_all(tiles, axis, 0, 0, tiled=True, axis_index_groups=groups)  35.8 us
    all_to_all x1, starting transfers between devices, on_device(): lax.all_to_all(tiles, 'stcol', 0, 0, tiled=True)  11.9 us
    pallas_call x1, Pallas kernels, on_device(): called(model_kernel, [model_out, state_out, ((STATIONS, STATIONS), BF16),...  7.06 us
    ppermute x3, starting transfers between devices, on_device(): lax.ppermute(send, 'freq', [(i, (i + 2 * d) % CHANNELS) for i in range(CH...  3.79 us
    ppermute x1, starting transfers between devices, on_device(): far = lax.ppermute(near, 'freq', [(i, i ^ 1) for i in range(CHANNELS)])  3.68 us
    all_to_all x1, starting transfers between devices, to_all(): lax.all_to_all(tiles, axis, 0, 0, tiled=True, axis_index_groups=groups)  3.49 us
    all_to_all x1, waiting for transfers between devices, to_all(): lax.all_to_all(tiles, axis, 0, 0, tiled=True, axis_index_groups=groups)  3.21 us
    pallas_call x1, Pallas kernels, on_device(): called(turn_kernel, [((STATIONS // OWN, 8, LANES), F32)], [((2 * OWN, 1,...  1.67 us
  transfers between devices with their start and end apart: 6, of which 2 were waited for; matrix products, arithmetic and copies ran while one was open for 2% of the time, Pallas kernels for 11%

profile of v2, /device:TPU:1, one launch (start us, length us, event | category | flops | bytes accessed | tf_op | source)
XLA Modules:
  0.0 80.2 jit_solution(4612708020730283665)
XLA Ops:
  0.6 1.7 %turn.1 = f32[32,8,128]{2,1,0:T(8,128)} custom-call(f32[32,1,512]{2,1,0:T(1,128)} %bitcast.26), custom_call_target="tpu_custom_call" | custom-call | tf_op jit(solution)/shard_map/turn/pallas_call | solution.py:437
  2.3 11.9 %all-to-all-start = ((f32[32,8,128]{2,1,0:T(8,128)}), f32[32,8,128]{2,1,0:T(8,128)S(1)}, u32[]{:S(2)}, u32[]{:S(2)}) async-start(f32[32,8,128]{2,1,0:T(8,128)} %turn.1), calls=%async_computation | async-start | bytes 262144 | tf_op jit(solution)/shard_map/all_to_all | solution.py:444
  14.2 0.8 reshape.46
  15.0 0.1 reshape.47.order_ref
  15.1 7.1 %models.1 = (f32[16,64,512]{2,1,0:T(8,128)S(1)}, f32[32,128]{1,0:T(8,128)S(1)}, bf16[512,512]{1,0:T(8,128)(2,1)S(1)}, f32[32,512]{1,0:T(8,128)S(1)}, f32[64,512]...) custom-call(f32[32,512]{1,0:T(8,128)} %bitcast.27, f32[3,1,512]{2,1,0:T(1,128)} %place_hbm.1, ...), custom_call_target="tpu_custom_call" | custom-call | tf_op jit(solution)/shard_map/models/pallas_call | solution.py:447
  22.2 1.2 %all-to-all-done = f32[32,8,128]{2,1,0:T(8,128)S(1)} async-done(((f32[32,8,128]{2,1,0:T(8,128)}), f32[32,8,128]{2,1,0:T(8,128)S(1)}, u32[]{:S(2)}, u32[]{:S(2)}) %all-to-all-start) | async-done | bytes 131104 | tf_op jit(solution)/shard_map/all_to_all | solution.py:444
  23.3 1.1 %pass_one.1 = (f32[64,512]{1,0:T(8,128)S(1)}, f32[32,128]{1,0:T(8,128)S(1)}, f32[8,128]{1,0:T(8,128)S(1)}) custom-call(f32[256,128]{1,0:T(8,128)S(1)} %bitcast.20, bf16[512,512]{1,0:T(8,128)(2,1)S(1)} %get-tuple-element.25.table_ref, f32[16,64,512]{2,1,0:T(8,128)S(1)} %get-tuple-element.24.model_ref, f32[32,512]{1,0:T(8,128)S(1)} %get-tuple-element.26.gains_ref, ...), custom_call_target="tpu_custom_call" | custom-call | tf_op jit(solution)/shard_map/pass_one/pallas_call | solution.py:461
  24.5 12.5 %all_to_all.25 = f32[16,8,128]{2,1,0:T(8,128)S(1)} all-to-all(f32[16,8,128]{2,1,0:T(8,128)S(1)} %broadcast_in_dim.12), channel_id=1, replica_groups={{0,1,2,3,8,9,10,11,16,17,18,19,24,25,26,27},{4,5,6,7,12,13,14,15,20,21,..., dimensions={0} | all-to-all | bytes 131072 | tf_op jit(solution)/shard_map/all_to_all | solution.py:419
  37.0 1.6 %pass_two.1 = (f32[32,128]{1,0:T(8,128)S(1)}, f32[8,128]{1,0:T(8,128)S(1)}) custom-call(f32[16,64,512]{2,1,0:T(8,128)S(1)} %get-tuple-element.24.model_ref, f32[64,512]{1,0:T(8,128)S(1)} %get-tuple-element.31.vis_ref, f32[128,128]{1,0:T(8,128)S(1)} %bitcast.23, f32[32,128]{1,0:T(8,128)S(1)} %get-tuple-element.33.own_ref, ...), custom_call_target="tpu_custom_call" | custom-call | tf_op jit(solution)/shard_map/pass_two/pallas_call | solution.py:465
  38.6 2.7 %collective-permute-start.2 = (f32[8,128]{1,0:T(8,128)S(1)}, f32[8,128]{1,0:T(8,128)S(1)}, u32[]{:S(2)}, u32[]{:S(2)}) collective-permute-start(f32[8,128]{1,0:T(8,128)S(1)} %get-tuple-element.34), channel_id=1, source_target_pairs={{0,192},{32,224},{64,0},{96,32},{128,64},{160,96},{192,128},{224,1... | collective-permute-start | bytes 12296 | tf_op jit(solution)/shard_map/ppermute | solution.py:469
  41.4 0.4 collective-permute-start.1
  41.7 0.7 collective-permute-start
  42.4 0.6 broadcast_in_dim.13
  43.0 3.5 %all-to-all-start.2 = ((f32[16,8,128]{2,1,0:T(8,128)}), f32[16,8,128]{2,1,0:T(8,128)S(1)}, u32[]{:S(2)}, u32[]{:S(2)}) async-start(f32[16,8,128]{2,1,0:T(8,128)} %broadcast_in_dim.13), calls=%async_computation.2 | async-start | bytes 131072 | tf_op jit(solution)/shard_map/all_to_all | solution.py:419
  46.5 0.0 collective-permute-done.1
  46.5 0.0 collective-permute-done
  46.6 3.7 %collective-permute-start.3 = (f32[4,8,128]{2,1,0:T(8,128)S(1)}, f32[4,8,128]{2,1,0:T(8,128)S(1)}, u32[]{:S(2)}, u32[]{:S(2)}) collective-permute-start(f32[4,8,128]{2,1,0:T(8,128)S(1)} %pad_maximum_fusion.near_ref), channel_id=1, source_target_pairs={{0,32},{32,0},{64,96},{96,64},{128,160},{160,128},{192,224},{224,1... | collective-permute-start | bytes 49160 | tf_op jit(solution)/shard_map/ppermute | solution.py:472
  50.2 3.2 %all-to-all-done.2 = f32[16,8,128]{2,1,0:T(8,128)S(1)} async-done(((f32[16,8,128]{2,1,0:T(8,128)}), f32[16,8,128]{2,1,0:T(8,128)S(1)}, u32[]{:S(2)}, u32[]{:S(2)}) %all-to-all-start.2) | async-done | bytes 65568 | tf_op jit(solution)/shard_map/all_to_all | solution.py:419
  53.5 1.6 %pass_three.1 = (f32[32,128]{1,0:T(8,128)S(1)}, f32[32,128]{1,0:T(8,128)S(1)}) custom-call(f32[16,64,512]{2,1,0:T(8,128)S(1)} %get-tuple-element.24.model_ref, f32[64,512]{1,0:T(8,128)S(1)} %get-tuple-element.31.vis_ref, f32[128,128]{1,0:T(8,128)S(1)} %bitcast.21, f32[32,128]{1,0:T(8,128)S(1)} %get-tuple-element.35.own_ref), custom_call_target="tpu_custom_call" | custom-call | tf_op jit(solution)/shard_map/pass_three/pallas_call | solution.py:474
  55.0 0.2 update_three.1
  55.2 10.7 %all_to_all.26 = f32[16,8,128]{2,1,0:T(8,128)S(1)} all-to-all(f32[16,8,128]{2,1,0:T(8,128)S(1)} %broadcast_in_dim.14), channel_id=1, replica_groups={{0,1,2,3,8,9,10,11,16,17,18,19,24,25,26,27},{4,5,6,7,12,13,14,15,20,21,..., dimensions={0} | all-to-all | bytes 131072 | tf_op jit(solution)/shard_map/all_to_all | solution.py:419
  66.0 0.9 %pass_four.1 = (f32[16,128]{1,0:T(8,128)S(1)}, f32[4,128]{1,0:T(4,128)S(1)}) custom-call(f32[16,64,512]{2,1,0:T(8,128)S(1)} %get-tuple-element.24.model_ref, f32[64,512]{1,0:T(8,128)S(1)} %get-tuple-element.31.vis_ref, f32[128,128]{1,0:T(8,128)S(1)} %bitcast.22, f32[32,128]{1,0:T(8,128)S(1)} %get-tuple-element.39.own_ref, ...), custom_call_target="tpu_custom_call" | custom-call | tf_op jit(solution)/shard_map/pass_four/pallas_call | solution.py:479
  66.9 12.5 %all_to_all.27.fit_ref = f32[8,4,128]{2,1,0:T(4,128)S(1)} all-to-all(f32[8,4,128]{2,1,0:T(4,128)S(1)} %broadcast_in_dim.15), channel_id=1, replica_groups=mesh['freq'=8,'stcol'=32] {'freq'}, dimensions={0} | all-to-all | bytes 32768 | tf_op jit(solution)/shard_map/all_to_all | solution.py:419
  79.4 0.8 consensus.1
  (7 shorter events, 0.0 us)
Async XLA Ops:
  2.3 21.0 %all-to-all-start = ((f32[32,8,128]{2,1,0:T(8,128)}), f32[32,8,128]{2,1,0:T(8,128)S(1)}, u32[]{:S(2)}, u32[]{:S(2)}) async-start(f32[32,8,128]{2,1,0:T(8,128)} %turn.1), calls=%async_computation | async-start | bytes 262144 | tf_op jit(solution)/shard_map/all_to_all | solution.py:444
  38.6 7.9 %collective-permute-start.2 = (f32[8,128]{1,0:T(8,128)S(1)}, f32[8,128]{1,0:T(8,128)S(1)}, u32[]{:S(2)}, u32[]{:S(2)}) collective-permute-start(f32[8,128]{1,0:T(8,128)S(1)} %get-tuple-element.34), channel_id=1, source_target_pairs={{0,192},{32,224},{64,0},{96,32},{128,64},{160,96},{192,128},{224,1... | collective-permute-start | bytes 12296 | tf_op jit(solution)/shard_map/ppermute | solution.py:469
  41.4 5.2 %collective-permute-start.1 = (f32[8,128]{1,0:T(8,128)S(1)}, f32[8,128]{1,0:T(8,128)S(1)}, u32[]{:S(2)}, u32[]{:S(2)}) collective-permute-start(f32[8,128]{1,0:T(8,128)S(1)} %get-tuple-element.34), channel_id=1, source_target_pairs={{0,128},{32,160},{64,192},{96,224},{128,0},{160,32},{192,64},{224,... | collective-permute-start | bytes 12296 | tf_op jit(solution)/shard_map/ppermute | solution.py:469
  41.7 4.8 %collective-permute-start = (f32[8,128]{1,0:T(8,128)S(1)}, f32[8,128]{1,0:T(8,128)S(1)}, u32[]{:S(2)}, u32[]{:S(2)}) collective-permute-start(f32[8,128]{1,0:T(8,128)S(1)} %get-tuple-element.34), channel_id=1, source_target_pairs={{0,64},{32,96},{64,128},{96,160},{128,192},{160,224},{192,0},{224,... | collective-permute-start | bytes 12296 | tf_op jit(solution)/shard_map/ppermute | solution.py:469
  43.0 10.4 %all-to-all-start.2 = ((f32[16,8,128]{2,1,0:T(8,128)}), f32[16,8,128]{2,1,0:T(8,128)S(1)}, u32[]{:S(2)}, u32[]{:S(2)}) async-start(f32[16,8,128]{2,1,0:T(8,128)} %broadcast_in_dim.13), calls=%async_computation.2 | async-start | bytes 131072 | tf_op jit(solution)/shard_map/all_to_all | solution.py:419
  46.6 8.5 %collective-permute-start.3 = (f32[4,8,128]{2,1,0:T(8,128)S(1)}, f32[4,8,128]{2,1,0:T(8,128)S(1)}, u32[]{:S(2)}, u32[]{:S(2)}) collective-permute-start(f32[4,8,128]{2,1,0:T(8,128)S(1)} %pad_maximum_fusion.near_ref), channel_id=1, source_target_pairs={{0,32},{32,0},{64,96},{96,64},{128,160},{160,128},{192,224},{224,1... | collective-permute-start | bytes 49160 | tf_op jit(solution)/shard_map/ppermute | solution.py:472

commit v3 on v2

--- a/solution.py
+++ b/solution.py
@@ -17,6 +17,8 @@
 ROWS = REPS * OWN
 MEMBERS = STATIONS // ROWS
 LANES = 128
+FRONT = 10
+LEAD = 31
 F32 = jnp.float32
 BF16 = jnp.bfloat16
 
@@ -69,13 +71,12 @@
     return (float(flat[0]), x * (1.0 / norm1), (x * x - lift * float(flat[0])) * (1.0 / norm2))
 
 
-def channel_weights(channel):
-    row = basis_row(channel)
-    return [sum(row[j] * float(BASIS[f, j]) for j in range(3)) for f in range(CHANNELS)]
-
-
 def channel_weight(channel, source):
     return sum(a * b for a, b in zip(basis_row(channel), basis_row(source)))
+
+
+def basis_product(channel, source):
+    return sum(a * float(b) for a, b in zip(basis_row(channel), BASIS[source]))
 
 
 def horner(u, terms):
@@ -130,7 +131,7 @@
 
 
 def station_at(place):
-    member = (place >> 3) & 15
+    member = ((place >> 3) & 15) ^ FRONT
     return ((member >> 2) << 7) + ((place >> 8) << 6) + ((member & 3) << 4) + (((place >> 7) & 1) << 3) + (place & 7)
 
 
@@ -173,7 +174,7 @@
                         moved = pltpu.roll(parts[2 * r + half], (to - (64 * a + 16 * b)) % LANES, 1)
                         tile = jnp.where((lane >> 4) == (to >> 4), moved, tile)
             for a in range(REPS):
-                tiles_ref[x * 8 + 4 * a + b] = tile
+                tiles_ref[(x * 8 + 4 * a + b) ^ LEAD] = tile
 
 
 def products(model_ref, gains_ref, start, k):
@@ -316,12 +317,15 @@
     return jnp.concatenate([turned[32 * a : 32 * a + 32, :] for a in range(4)], axis=1)
 
 
-def channel_fit(tiles_ref):
-    weights = channel_weights(lax.axis_index("freq"))
-    total = weights[0] * tiles_ref[0]
-    for f in range(1, CHANNELS):
-        total = total + weights[f] * tiles_ref[f]
-    return total
+def channel_fit(near_ref, far_ref):
+    channel = lax.axis_index("freq")
+    total = None
+    for d in range(CHANNELS // 2):
+        other = (channel - 2 * d) & (CHANNELS - 1)
+        for tiles_ref, source in ((near_ref, other), (far_ref, other ^ 1)):
+            part = channel_weight(channel, source) * tiles_ref[d]
+            total = part if total is None else total + part
+    return unpacked(total)
 
 
 def sums(model_ref, vis_ref, tiles_ref, own_ref, numer_ref, den_ref, along_ref, gains_ref):
@@ -359,14 +363,7 @@
 
 def anchor_kernel(numer_ref, den_ref, near_ref, far_ref, own_ref, penalty_ref, state_ref, anchor_ref, dual_ref, send_ref):
     own = own_ref[...]
-    channel = lax.axis_index("freq")
-    total = None
-    for d in range(CHANNELS // 2):
-        other = (channel - 2 * d) & (CHANNELS - 1)
-        for tiles_ref, source in ((near_ref, other), (far_ref, other ^ 1)):
-            part = channel_weight(channel, source) * tiles_ref[d]
-            total = part if total is None else total + part
-    cons = unpacked(total)
+    cons = channel_fit(near_ref, far_ref)
     dual = own - cons
     anchor = cons - dual
     state = updated(numer_ref[...], den_ref[...], own, anchor, penalty_ref[...])
@@ -394,9 +391,13 @@
     send_ref[...] = packed(state + dual_ref[rows, :])
 
 
-def last_kernel(fit_ref, state_ref, out_ref, cons_ref):
+def last_kernel(tiles_ref, state_ref, out_ref, cons_ref):
     out_ref[...] = by_direction(state_ref[...])
-    cons_ref[...] = by_direction(unpacked(channel_fit(fit_ref)))
+    channel = lax.axis_index("freq")
+    total = basis_product(channel, 0) * tiles_ref[0]
+    for f in range(1, CHANNELS):
+        total = total + basis_product(channel, f) * tiles_ref[f]
+    cons_ref[...] = by_direction(unpacked(total))
 
 
 def called(kernel, outs, scratch=(), name=None, in_specs=None):
@@ -419,8 +420,20 @@
     return lax.all_to_all(tiles, axis, 0, 0, tiled=True, axis_index_groups=groups)
 
 
+def around(tile):
+    return [tile] + [
+        lax.ppermute(tile, "freq", [(i, (i + 2 * d) % CHANNELS) for i in range(CHANNELS)]) for d in range(1, CHANNELS // 2)
+    ]
+
+
+def both_cores(tiles):
+    near = jnp.stack(tiles)
+    return near, lax.ppermute(near, "freq", [(i, i ^ 1) for i in range(CHANNELS)])
+
+
 def to_members(tile):
-    groups = [[x * 8 + 4 * m + b for x in range(4) for b in range(4)] for m in range(REPS)]
+    members = [e ^ FRONT for e in range(MEMBERS)]
+    groups = [[(e >> 2) * 8 + 4 * m + (e & 3) for e in members] for m in range(REPS)]
     return to_all(tile, "stcol", MEMBERS, groups).reshape(LANES, LANES)
 
 
@@ -441,8 +454,10 @@
         "turn",
         [hbm],
     )(held(visibilities.reshape(2 * OWN, 1, STATIONS)))
-    tiles = lax.all_to_all(tiles, "stcol", 0, 0, tiled=True).reshape(STATIONS // 2, LANES)
-    order = station_order.reshape(STATIONS // OWN, 2, 8).transpose(1, 0, 2).reshape(1, STATIONS)
+    slots = [s ^ LEAD for s in range(STATIONS // OWN)]
+    tiles = lax.all_to_all(tiles, "stcol", 0, 0, tiled=True, axis_index_groups=[slots]).reshape(STATIONS // 2, LANES)
+    order = station_order.reshape(STATIONS // OWN, 2, 8)
+    order = (order[::-1] if LEAD == 31 else order[jnp.array(slots)]).transpose(1, 0, 2).reshape(1, STATIONS)
     count = DIRS * SRC
     model, own, table, gains, pred, den, pen = called(
         model_kernel,
@@ -465,11 +480,7 @@
     state, send = called(second_kernel, [state_out, send_out], [along, gains_out, state_out], "pass_two")(
         model, vis, got, state, own, pen
     )
-    near = [send] + [
-        lax.ppermute(send, "freq", [(i, (i + 2 * d) % CHANNELS) for i in range(CHANNELS)]) for d in range(1, CHANNELS // 2)
-    ]
-    near = jnp.stack(near)
-    far = lax.ppermute(near, "freq", [(i, i ^ 1) for i in range(CHANNELS)])
+    near, far = both_cores(around(send))
     got = to_members(send)
     numer, den = called(sums, [state_out, state_out], [along, gains_out], "pass_three")(model, vis, got, state)
     state, anchor, dual, send = called(anchor_kernel, [state_out, state_out, state_out, send_out], name="update_three")(

time: 80.6 us -> 76.4 us (0.948)
  starting transfers between devices: 22.8 us -> 27.3 us
  blocking collectives: 35.8 us -> 31.4 us
  waiting for transfers between devices: 4.41 us -> 0.02 us
    all_to_all x3, blocking collectives: 35.8 us -> 31.4 us  [to_all(): lax.all_to_all(tiles, axis, 0, 0, tiled=True, axis_index_groups=groups)]
    all_to_all x1, waiting for transfers between devices: 3.21 us -> 0.01 us  [to_all(): lax.all_to_all(tiles, axis, 0, 0, tiled=True, axis_index_groups=groups)]
    all_to_all x1, starting transfers between devices: 3.49 us -> 6.63 us  [to_all(): lax.all_to_all(tiles, axis, 0, 0, tiled=True, axis_index_groups=groups)]
    all_to_all x1, waiting for transfers between devices: 1.19 us -> 0.01 us  [on_device(): lax.all_to_all(tiles, 'stcol', 0, 0, tiled=True, axis_index_groups=[slots])]
  transfers between devices with their start and end apart: 6 -> 6, of which waited for: 2 -> 0; matrix products, arithmetic and copies ran while one was open for 2% -> 2% of each run, Pallas kernels for 11% -> 11%
where the time goes in v3:
time: 76.4 us; the launch traced here: 75.9 us
  blocking collectives  31.4 us (41%)
  starting transfers between devices  27.3 us (36%)
  Pallas kernels  14.9 us (20%)
  local copies, waits for them, and re-layouts  1.54 us (2%)
    all_to_all x3, blocking collectives, to_all(): lax.all_to_all(tiles, axis, 0, 0, tiled=True, axis_index_groups=groups)  31.4 us
    all_to_all x1, starting transfers between devices, on_device(): lax.all_to_all(tiles, 'stcol', 0, 0, tiled=True, axis_index_groups=[slots])  12.6 us
    pallas_call x1, Pallas kernels, on_device(): called(model_kernel, [model_out, state_out, ((STATIONS, STATIONS), BF16),...  7.06 us
    all_to_all x1, starting transfers between devices, to_all(): lax.all_to_all(tiles, axis, 0, 0, tiled=True, axis_index_groups=groups)  6.63 us
    ppermute x1, starting transfers between devices, both_cores(): lax.ppermute(near, 'freq', [(i, i ^ 1) for i in range(CHANNELS)])  4.32 us
    ppermute x3, starting transfers between devices, around(): lax.ppermute(tile, 'freq', [(i, (i + 2 * d) % CHANNELS) for i in range(CH...  3.8 us
    pallas_call x1, Pallas kernels, on_device(): called(turn_kernel, [((STATIONS // OWN, 8, LANES), F32)], [((2 * OWN, 1,...  1.67 us
    pallas_call x1, Pallas kernels, on_device(): called(second_kernel, [state_out, send_out], [along, gains_out, state_out...  1.59 us
  transfers between devices with their start and end apart: 6, of which 0 were waited for; matrix products, arithmetic and copies ran while one was open for 2% of the time, Pallas kernels for 11%

profile of v3, /device:TPU:1, one launch (start us, length us, event | category | flops | bytes accessed | tf_op | source)
XLA Modules:
  0.0 75.9 jit_solution(9533369994481142844)
XLA Ops:
  0.6 1.7 %turn.1 = f32[32,8,128]{2,1,0:T(8,128)} custom-call(f32[32,1,512]{2,1,0:T(1,128)} %bitcast.26), custom_call_target="tpu_custom_call" | custom-call | tf_op jit(solution)/shard_map/turn/pallas_call | solution.py:450
  2.3 12.6 %all-to-all-start = ((f32[32,8,128]{2,1,0:T(8,128)}), f32[32,8,128]{2,1,0:T(8,128)S(1)}, u32[]{:S(2)}, u32[]{:S(2)}) async-start(f32[32,8,128]{2,1,0:T(8,128)} %turn.1), calls=%async_computation | async-start | bytes 262144 | tf_op jit(solution)/shard_map/all_to_all | solution.py:458
  14.9 0.8 %reshape.46 = s32[32,2,8]{2,1,0:T(2,128)S(1)} reshape(s32[512]{0:T(512)} %param.13) | data formatting | bytes 4096 | tf_op jit(solution)/shard_map/reshape | solution.py:459
  15.7 0.1 reshape.47.order_ref
  15.8 7.1 %models.1 = (f32[16,64,512]{2,1,0:T(8,128)S(1)}, f32[32,128]{1,0:T(8,128)S(1)}, bf16[512,512]{1,0:T(8,128)(2,1)S(1)}, f32[32,512]{1,0:T(8,128)S(1)}, f32[64,512]...) custom-call(f32[32,512]{1,0:T(8,128)} %bitcast.27, f32[3,1,512]{2,1,0:T(1,128)} %place_hbm.1, ...), custom_call_target="tpu_custom_call" | custom-call | tf_op jit(solution)/shard_map/models/pallas_call | solution.py:462
  22.9 0.0 all-to-all-done
  22.9 1.1 %pass_one.1 = (f32[64,512]{1,0:T(8,128)S(1)}, f32[32,128]{1,0:T(8,128)S(1)}, f32[8,128]{1,0:T(8,128)S(1)}) custom-call(f32[256,128]{1,0:T(8,128)S(1)} %bitcast.21, bf16[512,512]{1,0:T(8,128)(2,1)S(1)} %get-tuple-element.25.table_ref, f32[16,64,512]{2,1,0:T(8,128)S(1)} %get-tuple-element.24.model_ref, f32[32,512]{1,0:T(8,128)S(1)} %get-tuple-element.26.gains_ref, ...), custom_call_target="tpu_custom_call" | custom-call | tf_op jit(solution)/shard_map/pass_one/pallas_call | solution.py:476
  24.0 9.5 %all_to_all.25 = f32[16,8,128]{2,1,0:T(8,128)S(1)} all-to-all(f32[16,8,128]{2,1,0:T(8,128)S(1)} %broadcast_in_dim.12), channel_id=1, replica_groups={{18,19,16,17,26,27,24,25,2,3,0,1,10,11,8,9},{22,23,20,21,30,31,28,29,6,..., dimensions={0} | all-to-all | bytes 131072 | tf_op jit(solution)/shard_map/all_to_all | solution.py:420
  33.6 1.6 %pass_two.1 = (f32[32,128]{1,0:T(8,128)S(1)}, f32[8,128]{1,0:T(8,128)S(1)}) custom-call(f32[16,64,512]{2,1,0:T(8,128)S(1)} %get-tuple-element.24.model_ref, f32[64,512]{1,0:T(8,128)S(1)} %get-tuple-element.31.vis_ref, f32[128,128]{1,0:T(8,128)S(1)} %bitcast.24, f32[32,128]{1,0:T(8,128)S(1)} %get-tuple-element.33.own_ref, ...), custom_call_target="tpu_custom_call" | custom-call | tf_op jit(solution)/shard_map/pass_two/pallas_call | solution.py:480
  35.2 2.8 %collective-permute-start.2 = (f32[8,128]{1,0:T(8,128)S(1)}, f32[8,128]{1,0:T(8,128)S(1)}, u32[]{:S(2)}, u32[]{:S(2)}) collective-permute-start(f32[8,128]{1,0:T(8,128)S(1)} %get-tuple-element.34), channel_id=1, source_target_pairs={{0,192},{32,224},{64,0},{96,32},{128,64},{160,96},{192,128},{224,1... | collective-permute-start | bytes 12296 | tf_op jit(solution)/shard_map/ppermute | solution.py:425
  37.9 0.3 collective-permute-start.1
  38.3 0.7 collective-permute-start
  39.0 0.6 broadcast_in_dim.13
  39.6 6.6 %all-to-all-start.2 = ((f32[16,8,128]{2,1,0:T(8,128)}), f32[16,8,128]{2,1,0:T(8,128)S(1)}, u32[]{:S(2)}, u32[]{:S(2)}) async-start(f32[16,8,128]{2,1,0:T(8,128)} %broadcast_in_dim.13), calls=%async_computation.2 | async-start | bytes 131072 | tf_op jit(solution)/shard_map/all_to_all | solution.py:420
  46.2 0.0 collective-permute-done.2
  46.3 0.0 collective-permute-done
  46.3 4.3 %collective-permute-start.3 = (f32[4,8,128]{2,1,0:T(8,128)S(1)}, f32[4,8,128]{2,1,0:T(8,128)S(1)}, u32[]{:S(2)}, u32[]{:S(2)}) collective-permute-start(f32[4,8,128]{2,1,0:T(8,128)S(1)} %pad_maximum_fusion.near_ref), channel_id=1, source_target_pairs={{0,32},{32,0},{64,96},{96,64},{128,160},{160,128},{192,224},{224,1... | collective-permute-start | bytes 49160 | tf_op jit(solution)/shard_map/ppermute | solution.py:431
  50.6 0.0 all-to-all-done.2
  50.6 1.6 %pass_three.1 = (f32[32,128]{1,0:T(8,128)S(1)}, f32[32,128]{1,0:T(8,128)S(1)}) custom-call(f32[16,64,512]{2,1,0:T(8,128)S(1)} %get-tuple-element.24.model_ref, f32[64,512]{1,0:T(8,128)S(1)} %get-tuple-element.31.vis_ref, f32[128,128]{1,0:T(8,128)S(1)} %bitcast.22, f32[32,128]{1,0:T(8,128)S(1)} %get-tuple-element.35.own_ref), custom_call_target="tpu_custom_call" | custom-call | tf_op jit(solution)/shard_map/pass_three/pallas_call | solution.py:485
  52.2 0.2 update_three.1
  52.4 8.5 %all_to_all.26 = f32[16,8,128]{2,1,0:T(8,128)S(1)} all-to-all(f32[16,8,128]{2,1,0:T(8,128)S(1)} %broadcast_in_dim.14), channel_id=1, replica_groups={{18,19,16,17,26,27,24,25,2,3,0,1,10,11,8,9},{22,23,20,21,30,31,28,29,6,..., dimensions={0} | all-to-all | bytes 131072 | tf_op jit(solution)/shard_map/all_to_all | solution.py:420
  60.9 0.9 %pass_four.1 = (f32[16,128]{1,0:T(8,128)S(1)}, f32[4,128]{1,0:T(4,128)S(1)}) custom-call(f32[16,64,512]{2,1,0:T(8,128)S(1)} %get-tuple-element.24.model_ref, f32[64,512]{1,0:T(8,128)S(1)} %get-tuple-element.31.vis_ref, f32[128,128]{1,0:T(8,128)S(1)} %bitcast.23, f32[32,128]{1,0:T(8,128)S(1)} %get-tuple-element.39.own_ref, ...), custom_call_target="tpu_custom_call" | custom-call | tf_op jit(solution)/shard_map/pass_four/pallas_call | solution.py:490
  61.8 13.4 %all_to_all.27.tiles_ref = f32[8,4,128]{2,1,0:T(4,128)S(1)} all-to-all(f32[8,4,128]{2,1,0:T(4,128)S(1)} %broadcast_in_dim.15), channel_id=1, replica_groups=mesh['freq'=8,'stcol'=32] {'freq'}, dimensions={0} | all-to-all | bytes 32768 | tf_op jit(solution)/shard_map/all_to_all | solution.py:420
  75.2 0.8 %consensus.1 = (f32[32,16]{1,0:T(8,128)}, f32[32,16]{1,0:T(8,128)}) custom-call(f32[8,4,128]{2,1,0:T(4,128)S(1)} %all_to_all.27.tiles_ref, f32[16,128]{1,0:T(8,128)S(1)} %get-tuple-element.43.state_ref), custom_call_target="tpu_custom_call" | custom-call | tf_op jit(solution)/shard_map/consensus/pallas_call | solution.py:493
  (8 shorter events, 0.1 us)
Async XLA Ops:
  2.3 20.6 %all-to-all-start = ((f32[32,8,128]{2,1,0:T(8,128)}), f32[32,8,128]{2,1,0:T(8,128)S(1)}, u32[]{:S(2)}, u32[]{:S(2)}) async-start(f32[32,8,128]{2,1,0:T(8,128)} %turn.1), calls=%async_computation | async-start | bytes 262144 | tf_op jit(solution)/shard_map/all_to_all | solution.py:458
  35.2 11.1 %collective-permute-start.2 = (f32[8,128]{1,0:T(8,128)S(1)}, f32[8,128]{1,0:T(8,128)S(1)}, u32[]{:S(2)}, u32[]{:S(2)}) collective-permute-start(f32[8,128]{1,0:T(8,128)S(1)} %get-tuple-element.34), channel_id=1, source_target_pairs={{0,192},{32,224},{64,0},{96,32},{128,64},{160,96},{192,128},{224,1... | collective-permute-start | bytes 12296 | tf_op jit(solution)/shard_map/ppermute | solution.py:425
  37.9 8.3 %collective-permute-start.1 = (f32[8,128]{1,0:T(8,128)S(1)}, f32[8,128]{1,0:T(8,128)S(1)}, u32[]{:S(2)}, u32[]{:S(2)}) collective-permute-start(f32[8,128]{1,0:T(8,128)S(1)} %get-tuple-element.34), channel_id=1, source_target_pairs={{0,128},{32,160},{64,192},{96,224},{128,0},{160,32},{192,64},{224,... | collective-permute-start | bytes 12296 | tf_op jit(solution)/shard_map/ppermute | solution.py:425
  38.3 8.0 %collective-permute-start = (f32[8,128]{1,0:T(8,128)S(1)}, f32[8,128]{1,0:T(8,128)S(1)}, u32[]{:S(2)}, u32[]{:S(2)}) collective-permute-start(f32[8,128]{1,0:T(8,128)S(1)} %get-tuple-element.34), channel_id=1, source_target_pairs={{0,64},{32,96},{64,128},{96,160},{128,192},{160,224},{192,0},{224,... | collective-permute-start | bytes 12296 | tf_op jit(solution)/shard_map/ppermute | solution.py:425
  39.6 11.0 %all-to-all-start.2 = ((f32[16,8,128]{2,1,0:T(8,128)}), f32[16,8,128]{2,1,0:T(8,128)S(1)}, u32[]{:S(2)}, u32[]{:S(2)}) async-start(f32[16,8,128]{2,1,0:T(8,128)} %broadcast_in_dim.13), calls=%async_computation.2 | async-start | bytes 131072 | tf_op jit(solution)/shard_map/all_to_all | solution.py:420
  46.3 5.9 %collective-permute-start.3 = (f32[4,8,128]{2,1,0:T(8,128)S(1)}, f32[4,8,128]{2,1,0:T(8,128)S(1)}, u32[]{:S(2)}, u32[]{:S(2)}) collective-permute-start(f32[4,8,128]{2,1,0:T(8,128)S(1)} %pad_maximum_fusion.near_ref), channel_id=1, source_target_pairs={{0,32},{32,0},{64,96},{96,64},{128,160},{160,128},{192,224},{224,1... | collective-permute-start | bytes 49160 | tf_op jit(solution)/shard_map/ppermute | solution.py:431

commit v4 on v3

--- a/solution.py
+++ b/solution.py
@@ -19,6 +19,7 @@
 LANES = 128
 FRONT = 10
 LEAD = 31
+HEAD = 4
 F32 = jnp.float32
 BF16 = jnp.bfloat16
 
@@ -177,25 +178,22 @@
                 tiles_ref[(x * 8 + 4 * a + b) ^ LEAD] = tile
 
 
-def products(model_ref, gains_ref, start, k):
+def products(model_ref, gains_ref, start, k, lanes=slice(None)):
     half = model_ref.shape[1] // 2
-    model_real = model_ref[k, pl.ds(start, OWN), :]
-    model_imag = model_ref[k, pl.ds(start + half, OWN), :]
-    col_real = gains_ref[k : k + 1, :]
-    col_imag = gains_ref[DIRS + k : DIRS + k + 1, :]
+    model_real = model_ref[k, pl.ds(start, OWN), lanes]
+    model_imag = model_ref[k, pl.ds(start + half, OWN), lanes]
+    col_real = gains_ref[k : k + 1, lanes]
+    col_imag = gains_ref[DIRS + k : DIRS + k + 1, lanes]
     return model_real * col_real + model_imag * col_imag, model_imag * col_real - model_real * col_imag
 
 
-def predict(model_ref, gains_ref, own, start, along_ref):
+def predict(model_ref, gains_ref, own, start):
     pred_real = jnp.zeros((OWN, STATIONS), F32)
     pred_imag = jnp.zeros((OWN, STATIONS), F32)
     lane = iota((OWN, LANES), 1)
     denom = jnp.zeros((OWN, LANES), F32)
     for k in range(DIRS):
         along_real, along_imag = products(model_ref, gains_ref, start, k)
-        if along_ref is not None:
-            along_ref[k, 0:OWN, :] = along_real
-            along_ref[k, OWN : 2 * OWN, :] = along_imag
         row_real = own[:, k : k + 1]
         row_imag = own[:, DIRS + k : DIRS + k + 1]
         pred_real = pred_real + (row_real * along_real - row_imag * along_imag)
@@ -205,23 +203,66 @@
     return pred_real, pred_imag, denom
 
 
-def correlate(resid_real, resid_imag, along):
-    lane = iota((OWN, LANES), 1)
-    numer = jnp.zeros((OWN, LANES), F32)
+def lane_sums(part_ref):
+    shape = part_ref.shape
+    high, low = split2(part_ref[...].reshape(-1, LANES))
+    ones = jnp.ones((LANES, LANES), BF16)
+    return (dot(low, ones) + dot(high, ones)).reshape(shape)
+
+
+def by_lane(real, imag, rows):
+    lane = iota((rows, LANES), 1)
+    out = jnp.zeros((rows, LANES), F32)
     for k in range(DIRS):
-        along_real, along_imag = along(k)
-        num_real = jnp.sum(resid_real * along_real + resid_imag * along_imag, axis=1, keepdims=True)
-        num_imag = jnp.sum(resid_imag * along_real - resid_real * along_imag, axis=1, keepdims=True)
-        numer = jnp.where(lane == k, num_real, jnp.where(lane == DIRS + k, num_imag, numer))
-    return numer
-
-
-def row_sums(model_ref, vis_ref, gains_ref, own, start, along_ref):
-    pred_real, pred_imag, denom = predict(model_ref, gains_ref, own, start, along_ref)
-    resid_real = vis_ref[pl.ds(start, OWN), :] - pred_real
-    resid_imag = vis_ref[pl.ds(start + ROWS, OWN), :] - pred_imag
-    numer = correlate(resid_real, resid_imag, lambda k: (along_ref[k, 0:OWN, :], along_ref[k, OWN : 2 * OWN, :]))
-    return numer, denom
+        out = jnp.where(lane == k, real(k), jnp.where(lane == DIRS + k, imag(k), out))
+    return out
+
+
+def pieces_of(t):
+    return slice(t * LANES, (t + 1) * LANES)
+
+
+def row_sums(model_ref, vis_ref, turned, own, start, along_ref, part_ref):
+    n = own.shape[0]
+    real_rows, imag_rows = pl.ds(start, n), pl.ds(start + ROWS, n)
+    pred_real = [jnp.zeros((n, LANES), F32)] * 4
+    pred_imag = [jnp.zeros((n, LANES), F32)] * 4
+    for k in range(DIRS):
+        row_real = jnp.broadcast_to(own[:, k : k + 1], (n, LANES))
+        row_imag = jnp.broadcast_to(own[:, DIRS + k : DIRS + k + 1], (n, LANES))
+        squares = None
+        for t in range(4):
+            col_real = turned[32 * t + k : 32 * t + k + 1, :]
+            col_imag = turned[32 * t + DIRS + k : 32 * t + DIRS + k + 1, :]
+            model_real = model_ref[k, real_rows, pieces_of(t)]
+            model_imag = model_ref[k, imag_rows, pieces_of(t)]
+            along_real = model_real * col_real + model_imag * col_imag
+            along_imag = model_imag * col_real - model_real * col_imag
+            along_ref[k, 0:n, pieces_of(t)] = along_real
+            along_ref[k, n : 2 * n, pieces_of(t)] = along_imag
+            pred_real[t] = pred_real[t] + (row_real * along_real - row_imag * along_imag)
+            pred_imag[t] = pred_imag[t] + (row_real * along_imag + row_imag * along_real)
+            square = along_real * along_real + along_imag * along_imag
+            squares = square if squares is None else squares + square
+        part_ref[2, k] = squares
+    resid_real = [vis_ref[real_rows, pieces_of(t)] - pred_real[t] for t in range(4)]
+    resid_imag = [vis_ref[imag_rows, pieces_of(t)] - pred_imag[t] for t in range(4)]
+    correlate(resid_real, resid_imag, lambda k, t: (along_ref[k, 0:n, pieces_of(t)], along_ref[k, n : 2 * n, pieces_of(t)]), part_ref)
+    sums = lane_sums(part_ref)
+    return by_lane(lambda k: sums[0, k], lambda k: sums[1, k], n), by_lane(lambda k: sums[2, k], lambda k: sums[2, k], n)
+
+
+def correlate(resid_real, resid_imag, along, part_ref):
+    for k in range(DIRS):
+        real = imag = None
+        for t in range(4):
+            along_real, along_imag = along(k, t)
+            u = resid_real[t] * along_real + resid_imag[t] * along_imag
+            v = resid_imag[t] * along_real - resid_real[t] * along_imag
+            real = u if real is None else real + u
+            imag = v if imag is None else imag + v
+        part_ref[0, k] = real
+        part_ref[1, k] = imag
 
 
 def updated(numer, denom, own, anchor, penalty):
@@ -306,15 +347,10 @@
         model_ref[k, ROWS : 2 * ROWS, :] = jnp.where(kept, model[ROWS:, :], 0.0)
     for a in range(REPS):
         rows = slice(a * OWN, (a + 1) * OWN)
-        pred_real, pred_imag, denom = predict(model_ref, gains_ref, own_ref[rows, :], a * OWN, None)
+        pred_real, pred_imag, denom = predict(model_ref, gains_ref, own_ref[rows, :], a * OWN)
         pred_ref[rows, :] = pred_real
         pred_ref[ROWS + a * OWN : ROWS + (a + 1) * OWN, :] = pred_imag
         den_ref[rows, :] = denom
-
-
-def gathered_gains(tiles_ref):
-    turned = jnp.transpose(tiles_ref[...])
-    return jnp.concatenate([turned[32 * a : 32 * a + 32, :] for a in range(4)], axis=1)
 
 
 def channel_fit(near_ref, far_ref):
@@ -328,35 +364,38 @@
     return unpacked(total)
 
 
-def sums(model_ref, vis_ref, tiles_ref, own_ref, numer_ref, den_ref, along_ref, gains_ref):
-    gains_ref[...] = gathered_gains(tiles_ref)
-    for a in range(REPS):
-        rows = slice(a * OWN, (a + 1) * OWN)
-        numer, denom = row_sums(model_ref, vis_ref, gains_ref, own_ref[rows, :], a * OWN, along_ref)
-        numer_ref[rows, :] = numer
-        den_ref[rows, :] = denom
-
-
-def first_kernel(tiles_ref, table_ref, model_ref, gains_ref, pred_ref, den_ref, own_ref, penalty_ref, vis_ref, state_ref, send_ref):
+def sums(model_ref, vis_ref, tiles_ref, own_ref, numer_ref, den_ref, along_ref, part_ref):
+    turned = jnp.transpose(tiles_ref[...])
+    numer_ref[...], den_ref[...] = row_sums(model_ref, vis_ref, turned, own_ref[...], 0, along_ref, part_ref)
+
+
+def first_kernel(
+    tiles_ref, table_ref, model_ref, gains_ref, pred_ref, den_ref, own_ref, penalty_ref, vis_ref, state_ref, send_ref, part_ref
+):
     turned = jnp.transpose(tiles_ref[...])
     pieces = split3(jnp.concatenate([turned[0 : 2 * ROWS, :], turned[2 * ROWS :, :]], axis=1))
     vis_ref[...] = chosen(pieces, table_ref[...])
     for a in range(REPS):
         rows = slice(a * OWN, (a + 1) * OWN)
         lower = slice(ROWS + a * OWN, ROWS + (a + 1) * OWN)
-        resid_real = vis_ref[rows, :] - pred_ref[rows, :]
-        resid_imag = vis_ref[lower, :] - pred_ref[lower, :]
-        numer = correlate(resid_real, resid_imag, lambda k: products(model_ref, gains_ref, a * OWN, k))
-        own = own_ref[rows, :]
-        state_ref[rows, :] = updated(numer, den_ref[rows, :], own, own, penalty_ref[...])
-    send_ref[...] = packed(state_ref[...])
+        resid_real = [vis_ref[rows, pieces_of(t)] - pred_ref[rows, pieces_of(t)] for t in range(4)]
+        resid_imag = [vis_ref[lower, pieces_of(t)] - pred_ref[lower, pieces_of(t)] for t in range(4)]
+        correlate(resid_real, resid_imag, lambda k, t: products(model_ref, gains_ref, a * OWN, k, pieces_of(t)), part_ref.at[:, :, rows])
+    total = lane_sums(part_ref)
+    numer = by_lane(lambda k: total[0, k], lambda k: total[1, k], ROWS)
+    own = own_ref[...]
+    state = updated(numer, den_ref[...], own, own, penalty_ref[...])
+    state_ref[...] = state
+    send_ref[...] = packed(state)
 
 
 def second_kernel(
-    model_ref, vis_ref, tiles_ref, own_ref, anchor_ref, penalty_ref, state_ref, send_ref, along_ref, gains_ref, den_ref
+    model_ref, vis_ref, tiles_ref, own_ref, anchor_ref, penalty_ref, state_ref, send_ref, along_ref, part_ref
 ):
-    sums(model_ref, vis_ref, tiles_ref, own_ref, state_ref, den_ref, along_ref, gains_ref)
-    state = updated(state_ref[...], den_ref[...], own_ref[...], anchor_ref[...], penalty_ref[...])
+    turned = jnp.transpose(tiles_ref[...])
+    own = own_ref[...]
+    numer, denom = row_sums(model_ref, vis_ref, turned, own, 0, along_ref, part_ref)
+    state = updated(numer, denom, own, anchor_ref[...], penalty_ref[...])
     state_ref[...] = state
     send_ref[...] = packed(state)
 
@@ -379,13 +418,13 @@
 
 
 def fourth_kernel(
-    model_ref, vis_ref, tiles_ref, own_ref, anchor_ref, dual_ref, penalty_ref, state_ref, send_ref, along_ref, gains_ref
+    model_ref, vis_ref, tiles_ref, own_ref, anchor_ref, dual_ref, penalty_ref, state_ref, send_ref, along_ref, part_ref
 ):
     start = pl.multiple_of(rep_of(lax.axis_index("stcol")) * OWN, OWN)
     rows = pl.ds(start, OWN)
     own = own_ref[rows, :]
-    gains_ref[...] = gathered_gains(tiles_ref)
-    numer, denom = row_sums(model_ref, vis_ref, gains_ref, own, start, along_ref)
+    turned = jnp.transpose(tiles_ref[...])
+    numer, denom = row_sums(model_ref, vis_ref, turned, own, start, along_ref, part_ref)
     state = updated(numer, denom, own, anchor_ref[rows, :], penalty_ref[...])
     state_ref[...] = state
     send_ref[...] = packed(state + dual_ref[rows, :])
@@ -394,9 +433,9 @@
 def last_kernel(tiles_ref, state_ref, out_ref, cons_ref):
     out_ref[...] = by_direction(state_ref[...])
     channel = lax.axis_index("freq")
-    total = basis_product(channel, 0) * tiles_ref[0]
+    total = basis_product(channel, HEAD) * tiles_ref[0]
     for f in range(1, CHANNELS):
-        total = total + basis_product(channel, f) * tiles_ref[f]
+        total = total + basis_product(channel, f ^ HEAD) * tiles_ref[f]
     cons_ref[...] = by_direction(unpacked(total))
 
 
@@ -442,6 +481,8 @@
     vmem = pl.BlockSpec(memory_space=pltpu.VMEM)
     model_out = ((DIRS, 2 * ROWS, STATIONS), F32)
     along = ((DIRS, 2 * OWN, STATIONS), F32)
+    part = ((3, DIRS, OWN, LANES), F32)
+    parts = ((3, DIRS, ROWS, LANES), F32)
     vis_out = ((2 * ROWS, STATIONS), F32)
     state_out = ((ROWS, LANES), F32)
     send_out = ((ROWS // 4, LANES), F32)
@@ -473,24 +514,25 @@
         held(offsets.reshape(2 * DIRS, STATIONS)), held(positions), held(source_lmn), held(source_flux.reshape(1, count)),
         held(cluster_map.reshape(1, count)), order, held(penalty.reshape(1, DIRS)),
     )
-    vis, state, send = called(first_kernel, [vis_out, state_out, send_out], name="pass_one")(
+    vis, state, send = called(first_kernel, [vis_out, state_out, send_out], [((2, DIRS, ROWS, LANES), F32)], "pass_one")(
         tiles, table, model, gains, pred, den, own, pen
     )
     got = to_members(send)
-    state, send = called(second_kernel, [state_out, send_out], [along, gains_out, state_out], "pass_two")(
+    state, send = called(second_kernel, [state_out, send_out], [model_out, parts], "pass_two")(
         model, vis, got, state, own, pen
     )
-    near, far = both_cores(around(send))
+    tiles = around(send)
     got = to_members(send)
-    numer, den = called(sums, [state_out, state_out], [along, gains_out], "pass_three")(model, vis, got, state)
+    numer, den = called(sums, [state_out, state_out], [model_out, parts], "pass_three")(model, vis, got, state)
+    near, far = both_cores(lax.optimization_barrier((*tiles, got))[:-1])
     state, anchor, dual, send = called(anchor_kernel, [state_out, state_out, state_out, send_out], name="update_three")(
         numer, den, near, far, state, pen
     )
     got = to_members(send)
-    state, send = called(fourth_kernel, [((OWN, LANES), F32), ((4, LANES), F32)], [along, gains_out], "pass_four")(
+    state, send = called(fourth_kernel, [((OWN, LANES), F32), ((4, LANES), F32)], [along, part], "pass_four")(
         model, vis, got, state, anchor, dual, pen
     )
-    out, cons = called(last_kernel, [flat_out, flat_out], name="consensus")(to_all(send, "freq", CHANNELS), state)
+    out, cons = called(last_kernel, [flat_out, flat_out], name="consensus")(to_all(send, "freq", CHANNELS, [[f ^ HEAD for f in range(CHANNELS)]]), state)
     shape = (2, 1, DIRS, OWN)
     return out.reshape(shape), cons.reshape(shape)
 

time: 76.4 us -> 73.9 us (0.967)
  blocking collectives: 31.4 us -> 25.7 us
  waiting for transfers between devices: 0.02 us -> 2.98 us
  starting transfers between devices: 27.3 us -> 28.1 us
    all_to_all x3, blocking collectives: 31.4 us -> 25.7 us  [to_all(): lax.all_to_all(tiles, axis, 0, 0, tiled=True, axis_index_groups=groups)]
    ppermute x3, waiting for transfers between devices: 0.01 us -> 2.97 us  [around(): lax.ppermute(tile, 'freq', [(i, (i + 2 * d) % CHANNELS) for i in range(CH...]
    ppermute x1, starting transfers between devices: 4.32 us -> 5.11 us  [both_cores(): lax.ppermute(near, 'freq', [(i, i ^ 1) for i in range(CHANNELS)])]
  transfers between devices with their start and end apart: 6 -> 6, of which waited for: 0 -> 2; matrix products, arithmetic and copies ran while one was open for 2% -> 1% of each run, Pallas kernels for 11% -> 11%
where the time goes in v4:
time: 73.9 us; the launch traced here: 73.5 us
  starting transfers between devices  28.1 us (38%)
  blocking collectives  25.7 us (35%)
  Pallas kernels  14.4 us (19%)
  waiting for transfers between devices  2.98 us (4%)
  local copies, waits for them, and re-layouts  1.56 us (2%)
    all_to_all x3, blocking collectives, to_all(): lax.all_to_all(tiles, axis, 0, 0, tiled=True, axis_index_groups=groups)  25.7 us
    all_to_all x1, starting transfers between devices, on_device(): lax.all_to_all(tiles, 'stcol', 0, 0, tiled=True, axis_index_groups=[slots])  12.6 us
    pallas_call x1, Pallas kernels, on_device(): called(model_kernel, [model_out, state_out, ((STATIONS, STATIONS), BF16),...  7.06 us
    all_to_all x1, starting transfers between devices, to_all(): lax.all_to_all(tiles, axis, 0, 0, tiled=True, axis_index_groups=groups)  6.63 us
    ppermute x1, starting transfers between devices, both_cores(): lax.ppermute(near, 'freq', [(i, i ^ 1) for i in range(CHANNELS)])  5.11 us
    ppermute x3, starting transfers between devices, around(): lax.ppermute(tile, 'freq', [(i, (i + 2 * d) % CHANNELS) for i in range(CH...  3.78 us
    ppermute x3, waiting for transfers between devices, around(): lax.ppermute(tile, 'freq', [(i, (i + 2 * d) % CHANNELS) for i in range(CH...  2.97 us
    pallas_call x1, Pallas kernels, on_device(): called(turn_kernel, [((STATIONS // OWN, 8, LANES), F32)], [((2 * OWN, 1,...  1.67 us
  transfers between devices with their start and end apart: 6, of which 2 were waited for; matrix products, arithmetic and copies ran while one was open for 1% of the time, Pallas kernels for 11%

profile of v4, /device:TPU:1, one launch (start us, length us, event | category | flops | bytes accessed | tf_op | source)
XLA Modules:
  0.0 73.5 jit_solution(9168408591542837650)
XLA Ops:
  0.6 1.7 %turn.1 = f32[32,8,128]{2,1,0:T(8,128)} custom-call(f32[32,1,512]{2,1,0:T(1,128)} %bitcast.26), custom_call_target="tpu_custom_call" | custom-call | tf_op jit(solution)/shard_map/turn/pallas_call | solution.py:491
  2.3 12.6 %all-to-all-start = ((f32[32,8,128]{2,1,0:T(8,128)}), f32[32,8,128]{2,1,0:T(8,128)S(1)}, u32[]{:S(2)}, u32[]{:S(2)}) async-start(f32[32,8,128]{2,1,0:T(8,128)} %turn.1), calls=%async_computation | async-start | bytes 262144 | tf_op jit(solution)/shard_map/all_to_all | solution.py:499
  14.9 0.8 %reshape.46 = s32[32,2,8]{2,1,0:T(2,128)S(1)} reshape(s32[512]{0:T(512)} %param.13) | data formatting | bytes 4096 | tf_op jit(solution)/shard_map/reshape | solution.py:500
  15.7 0.1 reshape.47.order_ref
  15.8 7.1 %models.1 = (f32[16,64,512]{2,1,0:T(8,128)S(1)}, f32[32,128]{1,0:T(8,128)S(1)}, bf16[512,512]{1,0:T(8,128)(2,1)S(1)}, f32[32,512]{1,0:T(8,128)S(1)}, f32[64,512]...) custom-call(f32[32,512]{1,0:T(8,128)} %bitcast.27, f32[3,1,512]{2,1,0:T(1,128)} %place_hbm.1, ...), custom_call_target="tpu_custom_call" | custom-call | tf_op jit(solution)/shard_map/models/pallas_call | solution.py:503
  22.9 0.0 all-to-all-done
  22.9 1.3 %pass_one.1 = (f32[64,512]{1,0:T(8,128)S(1)}, f32[32,128]{1,0:T(8,128)S(1)}, f32[8,128]{1,0:T(8,128)S(1)}) custom-call(f32[256,128]{1,0:T(8,128)S(1)} %bitcast.21, bf16[512,512]{1,0:T(8,128)(2,1)S(1)} %get-tuple-element.29.table_ref, f32[16,64,512]{2,1,0:T(8,128)S(1)} %get-tuple-element.28.model_ref, f32[32,512]{1,0:T(8,128)S(1)} %get-tuple-element.30.gains_ref, ...), custom_call_target="tpu_custom_call" | custom-call | tf_op jit(solution)/shard_map/pass_one/pallas_call | solution.py:517
  24.2 9.5 %all_to_all.25 = f32[16,8,128]{2,1,0:T(8,128)S(1)} all-to-all(f32[16,8,128]{2,1,0:T(8,128)S(1)} %broadcast_in_dim.12), channel_id=1, replica_groups={{18,19,16,17,26,27,24,25,2,3,0,1,10,11,8,9},{22,23,20,21,30,31,28,29,6,..., dimensions={0} | all-to-all | bytes 131072 | tf_op jit(solution)/shard_map/all_to_all | solution.py:459
  33.7 1.3 %pass_two.1 = (f32[32,128]{1,0:T(8,128)S(1)}, f32[8,128]{1,0:T(8,128)S(1)}) custom-call(f32[16,64,512]{2,1,0:T(8,128)S(1)} %get-tuple-element.28.model_ref, f32[64,512]{1,0:T(8,128)S(1)} %get-tuple-element.35.vis_ref, f32[128,128]{1,0:T(8,128)S(1)} %bitcast.24, f32[32,128]{1,0:T(8,128)S(1)} %get-tuple-element.37.own_ref, ...), custom_call_target="tpu_custom_call" | custom-call | tf_op jit(solution)/shard_map/pass_two/pallas_call | solution.py:521
  35.0 0.6 broadcast_in_dim.13
  35.7 6.6 %all-to-all-start.2 = ((f32[16,8,128]{2,1,0:T(8,128)}), f32[16,8,128]{2,1,0:T(8,128)S(1)}, u32[]{:S(2)}, u32[]{:S(2)}) async-start(f32[16,8,128]{2,1,0:T(8,128)} %broadcast_in_dim.13), calls=%async_computation.2 | async-start | bytes 131072 | tf_op jit(solution)/shard_map/all_to_all | solution.py:459
  42.3 2.7 %collective-permute-start.2 = (f32[8,128]{1,0:T(8,128)S(1)}, f32[8,128]{1,0:T(8,128)S(1)}, u32[]{:S(2)}, u32[]{:S(2)}) collective-permute-start(f32[8,128]{1,0:T(8,128)S(1)} %get-tuple-element.42), channel_id=1, source_target_pairs={{0,192},{32,224},{64,0},{96,32},{128,64},{160,96},{192,128},{224,1... | collective-permute-start | bytes 12296 | tf_op jit(solution)/shard_map/ppermute | solution.py:464
  45.0 0.3 collective-permute-start.1
  45.4 0.7 collective-permute-start
  46.1 2.9 %collective-permute-done.1 = f32[8,128]{1,0:T(8,128)S(1)} collective-permute-done((f32[8,128]{1,0:T(8,128)S(1)}, f32[8,128]{1,0:T(8,128)S(1)}, u32[]{:S(2)}, u32[]{:S(2)}) %collective-permute-start.1) | collective-permute-done | bytes 4128 | tf_op jit(solution)/shard_map/ppermute | solution.py:464
  49.0 0.1 collective-permute-done
  49.1 5.1 %collective-permute-start.3 = (f32[4,8,128]{2,1,0:T(8,128)S(1)}, f32[4,8,128]{2,1,0:T(8,128)S(1)}, u32[]{:S(2)}, u32[]{:S(2)}) collective-permute-start(f32[4,8,128]{2,1,0:T(8,128)S(1)} %pad_maximum_fusion.near_ref), channel_id=1, source_target_pairs={{0,32},{32,0},{64,96},{96,64},{128,160},{160,128},{192,224},{224,1... | collective-permute-start | bytes 49160 | tf_op jit(solution)/shard_map/ppermute | solution.py:470
  54.2 1.2 %pass_three.1 = (f32[32,128]{1,0:T(8,128)S(1)}, f32[32,128]{1,0:T(8,128)S(1)}) custom-call(f32[16,64,512]{2,1,0:T(8,128)S(1)} %get-tuple-element.28.model_ref, f32[64,512]{1,0:T(8,128)S(1)} %get-tuple-element.35.vis_ref, f32[128,128]{1,0:T(8,128)S(1)} %bitcast.22, f32[32,128]{1,0:T(8,128)S(1)} %get-tuple-element.39.own_ref), custom_call_target="tpu_custom_call" | custom-call | tf_op jit(solution)/shard_map/pass_three/pallas_call | solution.py:526
  55.4 0.0 collective-permute-done.3.far_ref
  55.4 0.2 update_three.1
  55.6 8.6 %all_to_all.26 = f32[16,8,128]{2,1,0:T(8,128)S(1)} all-to-all(f32[16,8,128]{2,1,0:T(8,128)S(1)} %broadcast_in_dim.14), channel_id=1, replica_groups={{18,19,16,17,26,27,24,25,2,3,0,1,10,11,8,9},{22,23,20,21,30,31,28,29,6,..., dimensions={0} | all-to-all | bytes 131072 | tf_op jit(solution)/shard_map/all_to_all | solution.py:459
  64.3 0.9 %pass_four.1 = (f32[16,128]{1,0:T(8,128)S(1)}, f32[4,128]{1,0:T(4,128)S(1)}) custom-call(f32[16,64,512]{2,1,0:T(8,128)S(1)} %get-tuple-element.28.model_ref, f32[64,512]{1,0:T(8,128)S(1)} %get-tuple-element.35.vis_ref, f32[128,128]{1,0:T(8,128)S(1)} %bitcast.23, f32[32,128]{1,0:T(8,128)S(1)} %get-tuple-element.47.own_ref, ...), custom_call_target="tpu_custom_call" | custom-call | tf_op jit(solution)/shard_map/pass_four/pallas_call | solution.py:532
  65.1 7.6 %all_to_all.27.tiles_ref = f32[8,4,128]{2,1,0:T(4,128)S(1)} all-to-all(f32[8,4,128]{2,1,0:T(4,128)S(1)} %broadcast_in_dim.15), channel_id=1, replica_groups={{128,160,192,224,0,32,64,96},{129,161,193,225,1,33,65,97},{130,162,194,..., dimensions={0} | all-to-all | bytes 32768 | tf_op jit(solution)/shard_map/all_to_all | solution.py:459
  72.7 0.8 %consensus.1 = (f32[32,16]{1,0:T(8,128)}, f32[32,16]{1,0:T(8,128)}) custom-call(f32[8,4,128]{2,1,0:T(4,128)S(1)} %all_to_all.27.tiles_ref, f32[16,128]{1,0:T(8,128)S(1)} %get-tuple-element.51.state_ref), custom_call_target="tpu_custom_call" | custom-call | tf_op jit(solution)/shard_map/consensus/pallas_call | solution.py:535
  (8 shorter events, 0.1 us)
Async XLA Ops:
  2.3 20.6 %all-to-all-start = ((f32[32,8,128]{2,1,0:T(8,128)}), f32[32,8,128]{2,1,0:T(8,128)S(1)}, u32[]{:S(2)}, u32[]{:S(2)}) async-start(f32[32,8,128]{2,1,0:T(8,128)} %turn.1), calls=%async_computation | async-start | bytes 262144 | tf_op jit(solution)/shard_map/all_to_all | solution.py:499
  35.7 13.4 %all-to-all-start.2 = ((f32[16,8,128]{2,1,0:T(8,128)}), f32[16,8,128]{2,1,0:T(8,128)S(1)}, u32[]{:S(2)}, u32[]{:S(2)}) async-start(f32[16,8,128]{2,1,0:T(8,128)} %broadcast_in_dim.13), calls=%async_computation.2 | async-start | bytes 131072 | tf_op jit(solution)/shard_map/all_to_all | solution.py:459
  42.3 3.8 %collective-permute-start.2 = (f32[8,128]{1,0:T(8,128)S(1)}, f32[8,128]{1,0:T(8,128)S(1)}, u32[]{:S(2)}, u32[]{:S(2)}) collective-permute-start(f32[8,128]{1,0:T(8,128)S(1)} %get-tuple-element.42), channel_id=1, source_target_pairs={{0,192},{32,224},{64,0},{96,32},{128,64},{160,96},{192,128},{224,1... | collective-permute-start | bytes 12296 | tf_op jit(solution)/shard_map/ppermute | solution.py:464
  45.0 4.0 %collective-permute-start.1 = (f32[8,128]{1,0:T(8,128)S(1)}, f32[8,128]{1,0:T(8,128)S(1)}, u32[]{:S(2)}, u32[]{:S(2)}) collective-permute-start(f32[8,128]{1,0:T(8,128)S(1)} %get-tuple-element.42), channel_id=1, source_target_pairs={{0,128},{32,160},{64,192},{96,224},{128,0},{160,32},{192,64},{224,... | collective-permute-start | bytes 12296 | tf_op jit(solution)/shard_map/ppermute | solution.py:464
  45.4 3.7 %collective-permute-start = (f32[8,128]{1,0:T(8,128)S(1)}, f32[8,128]{1,0:T(8,128)S(1)}, u32[]{:S(2)}, u32[]{:S(2)}) collective-permute-start(f32[8,128]{1,0:T(8,128)S(1)} %get-tuple-element.42), channel_id=1, source_target_pairs={{0,64},{32,96},{64,128},{96,160},{128,192},{160,224},{192,0},{224,... | collective-permute-start | bytes 12296 | tf_op jit(solution)/shard_map/ppermute | solution.py:464
  49.1 6.4 %collective-permute-start.3 = (f32[4,8,128]{2,1,0:T(8,128)S(1)}, f32[4,8,128]{2,1,0:T(8,128)S(1)}, u32[]{:S(2)}, u32[]{:S(2)}) collective-permute-start(f32[4,8,128]{2,1,0:T(8,128)S(1)} %pad_maximum_fusion.near_ref), channel_id=1, source_target_pairs={{0,32},{32,0},{64,96},{96,64},{128,160},{160,128},{192,224},{224,1... | collective-permute-start | bytes 49160 | tf_op jit(solution)/shard_map/ppermute | solution.py:470

commit v5 on v4

--- a/solution.py
+++ b/solution.py
@@ -41,7 +41,7 @@
             out = poly.polyadd(poly.polymul(out, [-1.0, 8.0]), [c])
         return [float(np.float32(c)) for c in out[: degree + 1]]
 
-    return terms(np.cos(2 * np.pi * r), 7), terms(np.sin(2 * np.pi * r) / r, 6)
+    return terms(np.cos(2 * np.pi * r), 6), terms(np.sin(2 * np.pi * r) / r, 6)
 
 
 COS_TERMS, SIN_TERMS = fit_terms()
@@ -88,7 +88,7 @@
 
 
 def wrapped(turns):
-    return turns - jnp.round(turns)
+    return turns - ((turns + 12582912.0) - 12582912.0)
 
 
 def cos_turns(r):
@@ -271,13 +271,13 @@
 
 
 def model_kernel(
-    offs_hbm, place_hbm, lmn_hbm, flux_hbm, map_hbm, order_ref, penalty_hbm,
+    offs_hbm, place_hbm, lmn_hbm, flux_hbm, map_hbm, order_hbm, penalty_hbm,
     model_ref, own_ref, table_ref, gains_ref, pred_ref, den_ref, weight_ref,
-    offs_ref, xyz_ref, lmn_ref, flux_ref, map_ref, penalty_ref, sky_ref, part_ref, sems,
+    offs_ref, xyz_ref, lmn_ref, flux_ref, map_ref, order_ref, penalty_ref, sky_ref, part_ref, sems,
 ):
     pairs = [
         (map_hbm, map_ref), (lmn_hbm, lmn_ref), (flux_hbm, flux_ref),
-        (offs_hbm, offs_ref), (place_hbm, xyz_ref), (penalty_hbm, penalty_ref),
+        (offs_hbm, offs_ref), (place_hbm, xyz_ref), (penalty_hbm, penalty_ref), (order_hbm, order_ref),
     ]
     copies = [pltpu.make_async_copy(a, b, sems.at[n]) for n, (a, b) in enumerate(pairs)]
     for copy in copies:
@@ -297,7 +297,13 @@
     place = station_at(iota((STATIONS, STATIONS), 0))
     moved = chosen(pieces, as_table(place == iota((STATIONS, STATIONS), 1)))
     gains_ref[...] = moved[0 : 2 * DIRS, :]
-    table_ref[...] = as_table(place == order_ref[...])
+    column = iota((STATIONS, STATIONS), 0)
+    column = ((((column >> 3) & 31) ^ LEAD) << 4) + ((column >> 8) << 3) + (column & 7)
+    order = order_ref[...]
+    digits = jnp.concatenate([order >> 3, order & 7, jnp.zeros((6, STATIONS), jnp.int32)], axis=0).astype(F32)
+    digits = dot_nt(digits.astype(BF16), as_table(column == iota((STATIONS, STATIONS), 1)))
+    order = (8.0 * digits[0:1, :] + digits[1:2, :]).astype(jnp.int32)
+    table_ref[...] = as_table(place == order)
     mine = as_table(iota((ROWS, STATIONS), 1) == row_station((ROWS, STATIONS), 0, device))
     own = sum(dot_nt(mine, piece) for piece in pieces[::-1])
     own = jnp.concatenate([own, jnp.zeros((ROWS, LANES - own.shape[1]), F32)], axis=1)
@@ -357,7 +363,7 @@
     channel = lax.axis_index("freq")
     total = None
     for d in range(CHANNELS // 2):
-        other = (channel - 2 * d) & (CHANNELS - 1)
+        other = channel ^ (2 * d)
         for tiles_ref, source in ((near_ref, other), (far_ref, other ^ 1)):
             part = channel_weight(channel, source) * tiles_ref[d]
             total = part if total is None else total + part
@@ -380,13 +386,12 @@
         lower = slice(ROWS + a * OWN, ROWS + (a + 1) * OWN)
         resid_real = [vis_ref[rows, pieces_of(t)] - pred_ref[rows, pieces_of(t)] for t in range(4)]
         resid_imag = [vis_ref[lower, pieces_of(t)] - pred_ref[lower, pieces_of(t)] for t in range(4)]
-        correlate(resid_real, resid_imag, lambda k, t: products(model_ref, gains_ref, a * OWN, k, pieces_of(t)), part_ref.at[:, :, rows])
-    total = lane_sums(part_ref)
-    numer = by_lane(lambda k: total[0, k], lambda k: total[1, k], ROWS)
-    own = own_ref[...]
-    state = updated(numer, den_ref[...], own, own, penalty_ref[...])
-    state_ref[...] = state
-    send_ref[...] = packed(state)
+        correlate(resid_real, resid_imag, lambda k, t: products(model_ref, gains_ref, a * OWN, k, pieces_of(t)), part_ref)
+        total = [[jnp.sum(part_ref[r, k], axis=1, keepdims=True) for k in range(DIRS)] for r in range(2)]
+        numer = by_lane(lambda k: total[0][k], lambda k: total[1][k], OWN)
+        own = own_ref[rows, :]
+        state_ref[rows, :] = updated(numer, den_ref[rows, :], own, own, penalty_ref[...])
+    send_ref[...] = packed(state_ref[...])
 
 
 def second_kernel(
@@ -461,7 +466,7 @@
 
 def around(tile):
     return [tile] + [
-        lax.ppermute(tile, "freq", [(i, (i + 2 * d) % CHANNELS) for i in range(CHANNELS)]) for d in range(1, CHANNELS // 2)
+        lax.ppermute(tile, "freq", [(i, i ^ (2 * d)) for i in range(CHANNELS)]) for d in range(1, CHANNELS // 2)
     ]
 
 
@@ -478,7 +483,6 @@
 
 def on_device(visibilities, positions, source_lmn, source_flux, cluster_map, station_order, penalty, offsets):
     hbm = pl.BlockSpec(memory_space=pltpu.HBM)
-    vmem = pl.BlockSpec(memory_space=pltpu.VMEM)
     model_out = ((DIRS, 2 * ROWS, STATIONS), F32)
     along = ((DIRS, 2 * OWN, STATIONS), F32)
     part = ((3, DIRS, OWN, LANES), F32)
@@ -497,24 +501,22 @@
     )(held(visibilities.reshape(2 * OWN, 1, STATIONS)))
     slots = [s ^ LEAD for s in range(STATIONS // OWN)]
     tiles = lax.all_to_all(tiles, "stcol", 0, 0, tiled=True, axis_index_groups=[slots]).reshape(STATIONS // 2, LANES)
-    order = station_order.reshape(STATIONS // OWN, 2, 8)
-    order = (order[::-1] if LEAD == 31 else order[jnp.array(slots)]).transpose(1, 0, 2).reshape(1, STATIONS)
     count = DIRS * SRC
     model, own, table, gains, pred, den, pen = called(
         model_kernel,
         [model_out, state_out, ((STATIONS, STATIONS), BF16), gains_out, vis_out, state_out, ((1, LANES), F32)],
         [
             gains_out, ((3, 1, STATIONS), F32), ((3, count), F32), ((1, count), F32), ((1, count), jnp.int32),
-            pltpu.SMEM((1, DIRS), F32), ((4 * DIRS, 2 * SRC), F32), ((SRC, 4 * DIRS), F32),
-            pltpu.SemaphoreType.DMA((6,)),
+            ((1, STATIONS), jnp.int32), pltpu.SMEM((1, DIRS), F32), ((4 * DIRS, 2 * SRC), F32), ((SRC, 4 * DIRS), F32),
+            pltpu.SemaphoreType.DMA((7,)),
         ],
         "models",
-        [hbm, hbm, hbm, hbm, hbm, vmem, hbm],
+        [hbm] * 7,
     )(
         held(offsets.reshape(2 * DIRS, STATIONS)), held(positions), held(source_lmn), held(source_flux.reshape(1, count)),
-        held(cluster_map.reshape(1, count)), order, held(penalty.reshape(1, DIRS)),
-    )
-    vis, state, send = called(first_kernel, [vis_out, state_out, send_out], [((2, DIRS, ROWS, LANES), F32)], "pass_one")(
+        held(cluster_map.reshape(1, count)), held(station_order.reshape(1, STATIONS)), held(penalty.reshape(1, DIRS)),
+    )
+    vis, state, send = called(first_kernel, [vis_out, state_out, send_out], [((2, DIRS, OWN, LANES), F32)], "pass_one")(
         tiles, table, model, gains, pred, den, own, pen
     )
     got = to_members(send)

time: 73.9 us -> 72.6 us (0.982)
  local copies, waits for them, and re-layouts: 1.56 us -> 0.66 us
    reshape x2 -> x0, local copies, waits for them, and re-layouts: 0.88 us -> none  [the longest x1 0.79 us: on_device(): order = station_order.reshape(STATIONS // OWN, 2, 8)]
  transfers between devices with their start and end apart: 6 -> 6, of which waited for: 2 -> 2; matrix products, arithmetic and copies ran while one was open for 1% -> 0% of each run, Pallas kernels for 11% -> 11%
where the time goes in v5:
time: 72.6 us; the launch traced here: 72.2 us
  starting transfers between devices  27.6 us (38%)
  blocking collectives  25.7 us (35%)
  Pallas kernels  14.2 us (20%)
  waiting for transfers between devices  3.3 us (5%)
    all_to_all x3, blocking collectives, to_all(): lax.all_to_all(tiles, axis, 0, 0, tiled=True, axis_index_groups=groups)  25.7 us
    all_to_all x1, starting transfers between devices, on_device(): lax.all_to_all(tiles, 'stcol', 0, 0, tiled=True, axis_index_groups=[slots])  12.6 us
    pallas_call x1, Pallas kernels, on_device(): called(model_kernel, [model_out, state_out, ((STATIONS, STATIONS), BF16),...  7.07 us
    all_to_all x1, starting transfers between devices, to_all(): lax.all_to_all(tiles, axis, 0, 0, tiled=True, axis_index_groups=groups)  6.63 us
    ppermute x1, starting transfers between devices, both_cores(): lax.ppermute(near, 'freq', [(i, i ^ 1) for i in range(CHANNELS)])  4.92 us
    ppermute x3, starting transfers between devices, around(): lax.ppermute(tile, 'freq', [(i, i ^ 2 * d) for i in range(CHANNELS)])  3.41 us
    ppermute x3, waiting for transfers between devices, around(): lax.ppermute(tile, 'freq', [(i, i ^ 2 * d) for i in range(CHANNELS)])  3.29 us
    pallas_call x1, Pallas kernels, on_device(): called(turn_kernel, [((STATIONS // OWN, 8, LANES), F32)], [((2 * OWN, 1,...  1.67 us
  transfers between devices with their start and end apart: 6, of which 2 were waited for; matrix products, arithmetic and copies ran while one was open for 0% of the time, Pallas kernels for 11%

profile of v5, /device:TPU:1, one launch (start us, length us, event | category | flops | bytes accessed | tf_op | source)
XLA Modules:
  0.0 72.2 jit_solution(15197131401399753737)
XLA Ops:
  0.6 1.7 %turn.1 = f32[32,8,128]{2,1,0:T(8,128)} custom-call(f32[32,1,512]{2,1,0:T(1,128)} %bitcast.25), custom_call_target="tpu_custom_call" | custom-call | tf_op jit(solution)/shard_map/turn/pallas_call | solution.py:495
  2.3 12.6 %all-to-all-start = ((f32[32,8,128]{2,1,0:T(8,128)}), f32[32,8,128]{2,1,0:T(8,128)S(1)}, u32[]{:S(2)}, u32[]{:S(2)}) async-start(f32[32,8,128]{2,1,0:T(8,128)} %turn.1), calls=%async_computation | async-start | bytes 262144 | tf_op jit(solution)/shard_map/all_to_all | solution.py:503
  14.9 7.1 %models.1 = (f32[16,64,512]{2,1,0:T(8,128)S(1)}, f32[32,128]{1,0:T(8,128)S(1)}, bf16[512,512]{1,0:T(8,128)(2,1)S(1)}, f32[32,512]{1,0:T(8,128)S(1)}, f32[64,512]...) custom-call(f32[32,512]{1,0:T(8,128)} %bitcast.26, f32[3,1,512]{2,1,0:T(1,128)} %place_hbm.1, ...), custom_call_target="tpu_custom_call" | custom-call | tf_op jit(solution)/shard_map/models/pallas_call | solution.py:505
  22.0 0.0 all-to-all-done
  22.0 1.1 %pass_one.1 = (f32[64,512]{1,0:T(8,128)S(1)}, f32[32,128]{1,0:T(8,128)S(1)}, f32[8,128]{1,0:T(8,128)S(1)}) custom-call(f32[256,128]{1,0:T(8,128)S(1)} %bitcast.20, bf16[512,512]{1,0:T(8,128)(2,1)S(1)} %get-tuple-element.29.table_ref, f32[16,64,512]{2,1,0:T(8,128)S(1)} %get-tuple-element.28.model_ref, f32[32,512]{1,0:T(8,128)S(1)} %get-tuple-element.30.gains_ref, ...), custom_call_target="tpu_custom_call" | custom-call | tf_op jit(solution)/shard_map/pass_one/pallas_call | solution.py:519
  23.1 9.5 %all_to_all.25 = f32[16,8,128]{2,1,0:T(8,128)S(1)} all-to-all(f32[16,8,128]{2,1,0:T(8,128)S(1)} %broadcast_in_dim.12), channel_id=1, replica_groups={{18,19,16,17,26,27,24,25,2,3,0,1,10,11,8,9},{22,23,20,21,30,31,28,29,6,..., dimensions={0} | all-to-all | bytes 131072 | tf_op jit(solution)/shard_map/all_to_all | solution.py:464
  32.7 1.3 %pass_two.1 = (f32[32,128]{1,0:T(8,128)S(1)}, f32[8,128]{1,0:T(8,128)S(1)}) custom-call(f32[16,64,512]{2,1,0:T(8,128)S(1)} %get-tuple-element.28.model_ref, f32[64,512]{1,0:T(8,128)S(1)} %get-tuple-element.35.vis_ref, f32[128,128]{1,0:T(8,128)S(1)} %bitcast.23, f32[32,128]{1,0:T(8,128)S(1)} %get-tuple-element.37.own_ref, ...), custom_call_target="tpu_custom_call" | custom-call | tf_op jit(solution)/shard_map/pass_two/pallas_call | solution.py:523
  34.0 0.6 broadcast_in_dim.13
  34.6 6.6 %all-to-all-start.2 = ((f32[16,8,128]{2,1,0:T(8,128)}), f32[16,8,128]{2,1,0:T(8,128)S(1)}, u32[]{:S(2)}, u32[]{:S(2)}) async-start(f32[16,8,128]{2,1,0:T(8,128)} %broadcast_in_dim.13), calls=%async_computation.2 | async-start | bytes 131072 | tf_op jit(solution)/shard_map/all_to_all | solution.py:464
  41.2 2.7 %collective-permute-start.2 = (f32[8,128]{1,0:T(8,128)S(1)}, f32[8,128]{1,0:T(8,128)S(1)}, u32[]{:S(2)}, u32[]{:S(2)}) collective-permute-start(f32[8,128]{1,0:T(8,128)S(1)} %get-tuple-element.42), channel_id=1, source_target_pairs={{0,192},{32,224},{64,128},{96,160},{128,64},{160,96},{192,0},{224,... | collective-permute-start | bytes 12296 | tf_op jit(solution)/shard_map/ppermute | solution.py:469
  44.0 0.3 collective-permute-start.1
  44.3 0.3 collective-permute-start
  44.7 0.6 collective-permute-done.2
  45.3 2.7 %collective-permute-done.1 = f32[8,128]{1,0:T(8,128)S(1)} collective-permute-done((f32[8,128]{1,0:T(8,128)S(1)}, f32[8,128]{1,0:T(8,128)S(1)}, u32[]{:S(2)}, u32[]{:S(2)}) %collective-permute-start.1) | collective-permute-done | bytes 4128 | tf_op jit(solution)/shard_map/ppermute | solution.py:469
  47.9 0.0 collective-permute-done
  48.0 0.0 all-to-all-done.2
  48.0 4.9 %collective-permute-start.3 = (f32[4,8,128]{2,1,0:T(8,128)S(1)}, f32[4,8,128]{2,1,0:T(8,128)S(1)}, u32[]{:S(2)}, u32[]{:S(2)}) collective-permute-start(f32[4,8,128]{2,1,0:T(8,128)S(1)} %pad_maximum_fusion.near_ref), channel_id=1, source_target_pairs={{0,32},{32,0},{64,96},{96,64},{128,160},{160,128},{192,224},{224,1... | collective-permute-start | bytes 49160 | tf_op jit(solution)/shard_map/ppermute | solution.py:475
  52.9 1.2 %pass_three.1 = (f32[32,128]{1,0:T(8,128)S(1)}, f32[32,128]{1,0:T(8,128)S(1)}) custom-call(f32[16,64,512]{2,1,0:T(8,128)S(1)} %get-tuple-element.28.model_ref, f32[64,512]{1,0:T(8,128)S(1)} %get-tuple-element.35.vis_ref, f32[128,128]{1,0:T(8,128)S(1)} %bitcast.21, f32[32,128]{1,0:T(8,128)S(1)} %get-tuple-element.39.own_ref), custom_call_target="tpu_custom_call" | custom-call | tf_op jit(solution)/shard_map/pass_three/pallas_call | solution.py:528
  54.1 0.0 collective-permute-done.3.far_ref
  54.1 0.2 update_three.1
  54.3 8.6 %all_to_all.26 = f32[16,8,128]{2,1,0:T(8,128)S(1)} all-to-all(f32[16,8,128]{2,1,0:T(8,128)S(1)} %broadcast_in_dim.14), channel_id=1, replica_groups={{18,19,16,17,26,27,24,25,2,3,0,1,10,11,8,9},{22,23,20,21,30,31,28,29,6,..., dimensions={0} | all-to-all | bytes 131072 | tf_op jit(solution)/shard_map/all_to_all | solution.py:464
  63.0 0.9 %pass_four.1 = (f32[16,128]{1,0:T(8,128)S(1)}, f32[4,128]{1,0:T(4,128)S(1)}) custom-call(f32[16,64,512]{2,1,0:T(8,128)S(1)} %get-tuple-element.28.model_ref, f32[64,512]{1,0:T(8,128)S(1)} %get-tuple-element.35.vis_ref, f32[128,128]{1,0:T(8,128)S(1)} %bitcast.22, f32[32,128]{1,0:T(8,128)S(1)} %get-tuple-element.47.own_ref, ...), custom_call_target="tpu_custom_call" | custom-call | tf_op jit(solution)/shard_map/pass_four/pallas_call | solution.py:534
  63.8 7.6 %all_to_all.27.tiles_ref = f32[8,4,128]{2,1,0:T(4,128)S(1)} all-to-all(f32[8,4,128]{2,1,0:T(4,128)S(1)} %broadcast_in_dim.15), channel_id=1, replica_groups={{128,160,192,224,0,32,64,96},{129,161,193,225,1,33,65,97},{130,162,194,..., dimensions={0} | all-to-all | bytes 32768 | tf_op jit(solution)/shard_map/all_to_all | solution.py:464
  71.4 0.8 %consensus.1 = (f32[32,16]{1,0:T(8,128)}, f32[32,16]{1,0:T(8,128)}) custom-call(f32[8,4,128]{2,1,0:T(4,128)S(1)} %all_to_all.27.tiles_ref, f32[16,128]{1,0:T(8,128)S(1)} %get-tuple-element.51.state_ref), custom_call_target="tpu_custom_call" | custom-call | tf_op jit(solution)/shard_map/consensus/pallas_call | solution.py:537
  (4 shorter events, 0.0 us)
Async XLA Ops:
  2.3 19.7 %all-to-all-start = ((f32[32,8,128]{2,1,0:T(8,128)}), f32[32,8,128]{2,1,0:T(8,128)S(1)}, u32[]{:S(2)}, u32[]{:S(2)}) async-start(f32[32,8,128]{2,1,0:T(8,128)} %turn.1), calls=%async_computation | async-start | bytes 262144 | tf_op jit(solution)/shard_map/all_to_all | solution.py:503
  34.6 13.3 %all-to-all-start.2 = ((f32[16,8,128]{2,1,0:T(8,128)}), f32[16,8,128]{2,1,0:T(8,128)S(1)}, u32[]{:S(2)}, u32[]{:S(2)}) async-start(f32[16,8,128]{2,1,0:T(8,128)} %broadcast_in_dim.13), calls=%async_computation.2 | async-start | bytes 131072 | tf_op jit(solution)/shard_map/all_to_all | solution.py:464
  41.2 4.0 %collective-permute-start.2 = (f32[8,128]{1,0:T(8,128)S(1)}, f32[8,128]{1,0:T(8,128)S(1)}, u32[]{:S(2)}, u32[]{:S(2)}) collective-permute-start(f32[8,128]{1,0:T(8,128)S(1)} %get-tuple-element.42), channel_id=1, source_target_pairs={{0,192},{32,224},{64,128},{96,160},{128,64},{160,96},{192,0},{224,... | collective-permute-start | bytes 12296 | tf_op jit(solution)/shard_map/ppermute | solution.py:469
  44.0 4.0 %collective-permute-start.1 = (f32[8,128]{1,0:T(8,128)S(1)}, f32[8,128]{1,0:T(8,128)S(1)}, u32[]{:S(2)}, u32[]{:S(2)}) collective-permute-start(f32[8,128]{1,0:T(8,128)S(1)} %get-tuple-element.42), channel_id=1, source_target_pairs={{0,128},{32,160},{64,192},{96,224},{128,0},{160,32},{192,64},{224,... | collective-permute-start | bytes 12296 | tf_op jit(solution)/shard_map/ppermute | solution.py:469
  44.3 3.6 %collective-permute-start = (f32[8,128]{1,0:T(8,128)S(1)}, f32[8,128]{1,0:T(8,128)S(1)}, u32[]{:S(2)}, u32[]{:S(2)}) collective-permute-start(f32[8,128]{1,0:T(8,128)S(1)} %get-tuple-element.42), channel_id=1, source_target_pairs={{0,64},{32,96},{64,0},{96,32},{128,192},{160,224},{192,128},{224,1... | collective-permute-start | bytes 12296 | tf_op jit(solution)/shard_map/ppermute | solution.py:469
  48.0 6.2 %collective-permute-start.3 = (f32[4,8,128]{2,1,0:T(8,128)S(1)}, f32[4,8,128]{2,1,0:T(8,128)S(1)}, u32[]{:S(2)}, u32[]{:S(2)}) collective-permute-start(f32[4,8,128]{2,1,0:T(8,128)S(1)} %pad_maximum_fusion.near_ref), channel_id=1, source_target_pairs={{0,32},{32,0},{64,96},{96,64},{128,160},{160,128},{192,224},{224,1... | collective-permute-start | bytes 49160 | tf_op jit(solution)/shard_map/ppermute | solution.py:475

commit v6 on v5

--- a/solution.py
+++ b/solution.py
@@ -284,6 +284,13 @@
         copy.start()
     device = lax.axis_index("stcol")
     scale = 1.0 + 0.5 * lax.axis_index("freq").astype(F32) / CHANNELS
+    place = station_at(iota((STATIONS, STATIONS), 0))
+    placing = as_table(place == iota((STATIONS, STATIONS), 1))
+    column = iota((STATIONS, STATIONS), 0)
+    column = ((((column >> 3) & 31) ^ LEAD) << 4) + ((column >> 8) << 3) + (column & 7)
+    ordering = as_table(column == iota((STATIONS, STATIONS), 1))
+    mine = as_table(iota((ROWS, STATIONS), 1) == row_station((ROWS, STATIONS), 0, device))
+    ahead = as_table(iota((LANES, LANES), 0) <= iota((LANES, LANES), 1))
     for copy in copies:
         copy.wait()
     lane = iota((1, LANES), 1)
@@ -294,17 +301,13 @@
     offs = offs_ref[...]
     rows = [1.0 + offs[0:DIRS, :], offs[DIRS : 2 * DIRS, :]] + [xyz_ref[c] for c in range(3)]
     pieces = split3(jnp.concatenate(rows + [jnp.zeros((5, STATIONS), F32)], axis=0))
-    place = station_at(iota((STATIONS, STATIONS), 0))
-    moved = chosen(pieces, as_table(place == iota((STATIONS, STATIONS), 1)))
+    moved = chosen(pieces, placing)
     gains_ref[...] = moved[0 : 2 * DIRS, :]
-    column = iota((STATIONS, STATIONS), 0)
-    column = ((((column >> 3) & 31) ^ LEAD) << 4) + ((column >> 8) << 3) + (column & 7)
     order = order_ref[...]
     digits = jnp.concatenate([order >> 3, order & 7, jnp.zeros((6, STATIONS), jnp.int32)], axis=0).astype(F32)
-    digits = dot_nt(digits.astype(BF16), as_table(column == iota((STATIONS, STATIONS), 1)))
+    digits = dot_nt(digits.astype(BF16), ordering)
     order = (8.0 * digits[0:1, :] + digits[1:2, :]).astype(jnp.int32)
     table_ref[...] = as_table(place == order)
-    mine = as_table(iota((ROWS, STATIONS), 1) == row_station((ROWS, STATIONS), 0, device))
     own = sum(dot_nt(mine, piece) for piece in pieces[::-1])
     own = jnp.concatenate([own, jnp.zeros((ROWS, LANES - own.shape[1]), F32)], axis=1)
     own_xyz = [scale * own[:, 2 * DIRS + c : 2 * DIRS + c + 1] for c in range(3)]
@@ -314,7 +317,6 @@
     member_f = jnp.where(member, 1.0, 0.0)
     blocks = count // LANES
     stacked = jnp.concatenate([member_f[:, b * LANES : (b + 1) * LANES] for b in range(blocks)], axis=0)
-    ahead = as_table(iota((LANES, LANES), 0) <= iota((LANES, LANES), 1))
     running = dot(stacked.astype(BF16), ahead)
     carried = jnp.zeros((DIRS, 1), F32)
     ranks = []
@@ -465,9 +467,8 @@
 
 
 def around(tile):
-    return [tile] + [
-        lax.ppermute(tile, "freq", [(i, i ^ (2 * d)) for i in range(CHANNELS)]) for d in range(1, CHANNELS // 2)
-    ]
+    swaps = {d: lax.ppermute(tile, "freq", [(i, i ^ (2 * d)) for i in range(CHANNELS)]) for d in (1, 3, 2)}
+    return [tile, swaps[1], swaps[2], swaps[3]]
 
 
 def both_cores(tiles):

time: 72.6 us -> 72.5 us (level)
  no operation moved by 1% of the time
where the time goes in v6:
time: 72.5 us; the launch traced here: 72 us
  starting transfers between devices  27.6 us (38%)
  blocking collectives  25.7 us (35%)
  Pallas kernels  14.1 us (19%)
  waiting for transfers between devices  3.3 us (5%)
    all_to_all x3, blocking collectives, to_all(): lax.all_to_all(tiles, axis, 0, 0, tiled=True, axis_index_groups=groups)  25.7 us
    all_to_all x1, starting transfers between devices, on_device(): lax.all_to_all(tiles, 'stcol', 0, 0, tiled=True, axis_index_groups=[slots])  12.6 us
    pallas_call x1, Pallas kernels, on_device(): called(model_kernel, [model_out, state_out, ((STATIONS, STATIONS), BF16),...  6.93 us
    all_to_all x1, starting transfers between devices, to_all(): lax.all_to_all(tiles, axis, 0, 0, tiled=True, axis_index_groups=groups)  6.63 us
    ppermute x1, starting transfers between devices, both_cores(): lax.ppermute(near, 'freq', [(i, i ^ 1) for i in range(CHANNELS)])  4.92 us
    ppermute x3, starting transfers between devices, around(): lax.ppermute(tile, 'freq', [(i, i ^ 2 * d) for i in range(CHANNELS)])  3.4 us
    ppermute x3, waiting for transfers between devices, around(): lax.ppermute(tile, 'freq', [(i, i ^ 2 * d) for i in range(CHANNELS)])  3.29 us
    pallas_call x1, Pallas kernels, on_device(): called(turn_kernel, [((STATIONS // OWN, 8, LANES), F32)], [((2 * OWN, 1,...  1.67 us
  transfers between devices with their start and end apart: 6, of which 2 were waited for; matrix products, arithmetic and copies ran while one was open for 0% of the time, Pallas kernels for 11%

profile of v6, /device:TPU:1, one launch (start us, length us, event | category | flops | bytes accessed | tf_op | source)
XLA Modules:
  0.0 72.0 jit_solution(7796857138105830457)
XLA Ops:
  0.6 1.7 %turn.1 = f32[32,8,128]{2,1,0:T(8,128)} custom-call(f32[32,1,512]{2,1,0:T(1,128)} %bitcast.25), custom_call_target="tpu_custom_call" | custom-call | tf_op jit(solution)/shard_map/turn/pallas_call | solution.py:496
  2.3 12.6 %all-to-all-start = ((f32[32,8,128]{2,1,0:T(8,128)}), f32[32,8,128]{2,1,0:T(8,128)S(1)}, u32[]{:S(2)}, u32[]{:S(2)}) async-start(f32[32,8,128]{2,1,0:T(8,128)} %turn.1), calls=%async_computation | async-start | bytes 262144 | tf_op jit(solution)/shard_map/all_to_all | solution.py:504
  14.9 6.9 %models.1 = (f32[16,64,512]{2,1,0:T(8,128)S(1)}, f32[32,128]{1,0:T(8,128)S(1)}, bf16[512,512]{1,0:T(8,128)(2,1)S(1)}, f32[32,512]{1,0:T(8,128)S(1)}, f32[64,512]...) custom-call(f32[32,512]{1,0:T(8,128)} %bitcast.26, f32[3,1,512]{2,1,0:T(1,128)} %place_hbm.1, ...), custom_call_target="tpu_custom_call" | custom-call | tf_op jit(solution)/shard_map/models/pallas_call | solution.py:506
  21.8 0.0 all-to-all-done
  21.9 1.1 %pass_one.1 = (f32[64,512]{1,0:T(8,128)S(1)}, f32[32,128]{1,0:T(8,128)S(1)}, f32[8,128]{1,0:T(8,128)S(1)}) custom-call(f32[256,128]{1,0:T(8,128)S(1)} %bitcast.20, bf16[512,512]{1,0:T(8,128)(2,1)S(1)} %get-tuple-element.29.table_ref, f32[16,64,512]{2,1,0:T(8,128)S(1)} %get-tuple-element.28.model_ref, f32[32,512]{1,0:T(8,128)S(1)} %get-tuple-element.30.gains_ref, ...), custom_call_target="tpu_custom_call" | custom-call | tf_op jit(solution)/shard_map/pass_one/pallas_call | solution.py:520
  23.0 9.5 %all_to_all.25 = f32[16,8,128]{2,1,0:T(8,128)S(1)} all-to-all(f32[16,8,128]{2,1,0:T(8,128)S(1)} %broadcast_in_dim.12), channel_id=1, replica_groups={{18,19,16,17,26,27,24,25,2,3,0,1,10,11,8,9},{22,23,20,21,30,31,28,29,6,..., dimensions={0} | all-to-all | bytes 131072 | tf_op jit(solution)/shard_map/all_to_all | solution.py:466
  32.5 1.3 %pass_two.1 = (f32[32,128]{1,0:T(8,128)S(1)}, f32[8,128]{1,0:T(8,128)S(1)}) custom-call(f32[16,64,512]{2,1,0:T(8,128)S(1)} %get-tuple-element.28.model_ref, f32[64,512]{1,0:T(8,128)S(1)} %get-tuple-element.35.vis_ref, f32[128,128]{1,0:T(8,128)S(1)} %bitcast.23, f32[32,128]{1,0:T(8,128)S(1)} %get-tuple-element.37.own_ref, ...), custom_call_target="tpu_custom_call" | custom-call | tf_op jit(solution)/shard_map/pass_two/pallas_call | solution.py:524
  33.8 0.6 broadcast_in_dim.13
  34.5 6.6 %all-to-all-start.2 = ((f32[16,8,128]{2,1,0:T(8,128)}), f32[16,8,128]{2,1,0:T(8,128)S(1)}, u32[]{:S(2)}, u32[]{:S(2)}) async-start(f32[16,8,128]{2,1,0:T(8,128)} %broadcast_in_dim.13), calls=%async_computation.2 | async-start | bytes 131072 | tf_op jit(solution)/shard_map/all_to_all | solution.py:466
  41.1 2.7 %collective-permute-start.2 = (f32[8,128]{1,0:T(8,128)S(1)}, f32[8,128]{1,0:T(8,128)S(1)}, u32[]{:S(2)}, u32[]{:S(2)}) collective-permute-start(f32[8,128]{1,0:T(8,128)S(1)} %get-tuple-element.42), channel_id=1, source_target_pairs={{0,192},{32,224},{64,128},{96,160},{128,64},{160,96},{192,0},{224,... | collective-permute-start | bytes 12296 | tf_op jit(solution)/shard_map/ppermute | solution.py:470
  43.8 0.3 collective-permute-start.1
  44.2 0.3 collective-permute-start
  44.5 0.6 collective-permute-done.2
  45.1 2.7 %collective-permute-done.1 = f32[8,128]{1,0:T(8,128)S(1)} collective-permute-done((f32[8,128]{1,0:T(8,128)S(1)}, f32[8,128]{1,0:T(8,128)S(1)}, u32[]{:S(2)}, u32[]{:S(2)}) %collective-permute-start.1) | collective-permute-done | bytes 4128 | tf_op jit(solution)/shard_map/ppermute | solution.py:470
  47.8 0.0 collective-permute-done
  47.8 0.0 all-to-all-done.2
  47.8 4.9 %collective-permute-start.3 = (f32[4,8,128]{2,1,0:T(8,128)S(1)}, f32[4,8,128]{2,1,0:T(8,128)S(1)}, u32[]{:S(2)}, u32[]{:S(2)}) collective-permute-start(f32[4,8,128]{2,1,0:T(8,128)S(1)} %pad_maximum_fusion.near_ref), channel_id=1, source_target_pairs={{0,32},{32,0},{64,96},{96,64},{128,160},{160,128},{192,224},{224,1... | collective-permute-start | bytes 49160 | tf_op jit(solution)/shard_map/ppermute | solution.py:476
  52.7 1.2 %pass_three.1 = (f32[32,128]{1,0:T(8,128)S(1)}, f32[32,128]{1,0:T(8,128)S(1)}) custom-call(f32[16,64,512]{2,1,0:T(8,128)S(1)} %get-tuple-element.28.model_ref, f32[64,512]{1,0:T(8,128)S(1)} %get-tuple-element.35.vis_ref, f32[128,128]{1,0:T(8,128)S(1)} %bitcast.21, f32[32,128]{1,0:T(8,128)S(1)} %get-tuple-element.39.own_ref), custom_call_target="tpu_custom_call" | custom-call | tf_op jit(solution)/shard_map/pass_three/pallas_call | solution.py:529
  54.0 0.0 collective-permute-done.3.far_ref
  54.0 0.2 update_three.1
  54.2 8.6 %all_to_all.26 = f32[16,8,128]{2,1,0:T(8,128)S(1)} all-to-all(f32[16,8,128]{2,1,0:T(8,128)S(1)} %broadcast_in_dim.14), channel_id=1, replica_groups={{18,19,16,17,26,27,24,25,2,3,0,1,10,11,8,9},{22,23,20,21,30,31,28,29,6,..., dimensions={0} | all-to-all | bytes 131072 | tf_op jit(solution)/shard_map/all_to_all | solution.py:466
  62.8 0.9 %pass_four.1 = (f32[16,128]{1,0:T(8,128)S(1)}, f32[4,128]{1,0:T(4,128)S(1)}) custom-call(f32[16,64,512]{2,1,0:T(8,128)S(1)} %get-tuple-element.28.model_ref, f32[64,512]{1,0:T(8,128)S(1)} %get-tuple-element.35.vis_ref, f32[128,128]{1,0:T(8,128)S(1)} %bitcast.22, f32[32,128]{1,0:T(8,128)S(1)} %get-tuple-element.47.own_ref, ...), custom_call_target="tpu_custom_call" | custom-call | tf_op jit(solution)/shard_map/pass_four/pallas_call | solution.py:535
  63.7 7.6 %all_to_all.27.tiles_ref = f32[8,4,128]{2,1,0:T(4,128)S(1)} all-to-all(f32[8,4,128]{2,1,0:T(4,128)S(1)} %broadcast_in_dim.15), channel_id=1, replica_groups={{128,160,192,224,0,32,64,96},{129,161,193,225,1,33,65,97},{130,162,194,..., dimensions={0} | all-to-all | bytes 32768 | tf_op jit(solution)/shard_map/all_to_all | solution.py:466
  71.3 0.8 %consensus.1 = (f32[32,16]{1,0:T(8,128)}, f32[32,16]{1,0:T(8,128)}) custom-call(f32[8,4,128]{2,1,0:T(4,128)S(1)} %all_to_all.27.tiles_ref, f32[16,128]{1,0:T(8,128)S(1)} %get-tuple-element.51.state_ref), custom_call_target="tpu_custom_call" | custom-call | tf_op jit(solution)/shard_map/consensus/pallas_call | solution.py:538
  (4 shorter events, 0.0 us)
Async XLA Ops:
  2.3 19.5 %all-to-all-start = ((f32[32,8,128]{2,1,0:T(8,128)}), f32[32,8,128]{2,1,0:T(8,128)S(1)}, u32[]{:S(2)}, u32[]{:S(2)}) async-start(f32[32,8,128]{2,1,0:T(8,128)} %turn.1), calls=%async_computation | async-start | bytes 262144 | tf_op jit(solution)/shard_map/all_to_all | solution.py:504
  34.5 13.3 %all-to-all-start.2 = ((f32[16,8,128]{2,1,0:T(8,128)}), f32[16,8,128]{2,1,0:T(8,128)S(1)}, u32[]{:S(2)}, u32[]{:S(2)}) async-start(f32[16,8,128]{2,1,0:T(8,128)} %broadcast_in_dim.13), calls=%async_computation.2 | async-start | bytes 131072 | tf_op jit(solution)/shard_map/all_to_all | solution.py:466
  41.1 4.0 %collective-permute-start.2 = (f32[8,128]{1,0:T(8,128)S(1)}, f32[8,128]{1,0:T(8,128)S(1)}, u32[]{:S(2)}, u32[]{:S(2)}) collective-permute-start(f32[8,128]{1,0:T(8,128)S(1)} %get-tuple-element.42), channel_id=1, source_target_pairs={{0,192},{32,224},{64,128},{96,160},{128,64},{160,96},{192,0},{224,... | collective-permute-start | bytes 12296 | tf_op jit(solution)/shard_map/ppermute | solution.py:470
  43.8 4.0 %collective-permute-start.1 = (f32[8,128]{1,0:T(8,128)S(1)}, f32[8,128]{1,0:T(8,128)S(1)}, u32[]{:S(2)}, u32[]{:S(2)}) collective-permute-start(f32[8,128]{1,0:T(8,128)S(1)} %get-tuple-element.42), channel_id=1, source_target_pairs={{0,128},{32,160},{64,192},{96,224},{128,0},{160,32},{192,64},{224,... | collective-permute-start | bytes 12296 | tf_op jit(solution)/shard_map/ppermute | solution.py:470
  44.2 3.6 %collective-permute-start = (f32[8,128]{1,0:T(8,128)S(1)}, f32[8,128]{1,0:T(8,128)S(1)}, u32[]{:S(2)}, u32[]{:S(2)}) collective-permute-start(f32[8,128]{1,0:T(8,128)S(1)} %get-tuple-element.42), channel_id=1, source_target_pairs={{0,64},{32,96},{64,0},{96,32},{128,192},{160,224},{192,128},{224,1... | collective-permute-start | bytes 12296 | tf_op jit(solution)/shard_map/ppermute | solution.py:470
  47.8 6.2 %collective-permute-start.3 = (f32[4,8,128]{2,1,0:T(8,128)S(1)}, f32[4,8,128]{2,1,0:T(8,128)S(1)}, u32[]{:S(2)}, u32[]{:S(2)}) collective-permute-start(f32[4,8,128]{2,1,0:T(8,128)S(1)} %pad_maximum_fusion.near_ref), channel_id=1, source_target_pairs={{0,32},{32,0},{64,96},{96,64},{128,160},{160,128},{192,224},{224,1... | collective-permute-start | bytes 49160 | tf_op jit(solution)/shard_map/ppermute | solution.py:476

commit v7 on v6

--- a/solution.py
+++ b/solution.py
@@ -159,10 +159,11 @@
     return jnp.where(iota(both.shape, 1) < 2 * DIRS, both, 0.0)
 
 
-def turn_kernel(vis_hbm, tiles_ref, vis_ref, sem):
-    copy = pltpu.make_async_copy(vis_hbm, vis_ref, sem)
+def turn_kernel(vis_hbm, tiles_hbm, vis_ref, tiles_ref, sems):
+    copy = pltpu.make_async_copy(vis_hbm, vis_ref, sems.at[4])
     copy.start()
     copy.wait()
+    going = [pltpu.make_async_copy(tiles_ref.at[x], tiles_hbm.at[x], sems.at[x]) for x in range(4)]
     lane = iota((8, LANES), 1)
     for x in range(4):
         parts = [vis_ref[r * 8 : (r + 1) * 8, 0, x * LANES : (x + 1) * LANES] for r in range(4)]
@@ -175,7 +176,10 @@
                         moved = pltpu.roll(parts[2 * r + half], (to - (64 * a + 16 * b)) % LANES, 1)
                         tile = jnp.where((lane >> 4) == (to >> 4), moved, tile)
             for a in range(REPS):
-                tiles_ref[(x * 8 + 4 * a + b) ^ LEAD] = tile
+                tiles_ref[x ^ (LEAD >> 3), (4 * a + b) ^ (LEAD & 7)] = tile
+        going[x ^ (LEAD >> 3)].start()
+    for copy in going:
+        copy.wait()
 
 
 def products(model_ref, gains_ref, start, k, lanes=slice(None)):
@@ -446,7 +450,7 @@
     cons_ref[...] = by_direction(unpacked(total))
 
 
-def called(kernel, outs, scratch=(), name=None, in_specs=None):
+def called(kernel, outs, scratch=(), name=None, in_specs=None, out_specs=None):
     return pl.pallas_call(
         kernel,
         out_shape=[jax.ShapeDtypeStruct(*o) for o in outs],
@@ -454,6 +458,7 @@
         compiler_params=pltpu.CompilerParams(vmem_limit_bytes=32 * 1024 * 1024),
         name=name,
         **({} if in_specs is None else {"in_specs": in_specs}),
+        **({} if out_specs is None else {"out_specs": out_specs}),
     )
 
 
@@ -495,13 +500,14 @@
     gains_out = ((2 * DIRS, STATIONS), F32)
     (tiles,) = called(
         turn_kernel,
-        [((STATIONS // OWN, 8, LANES), F32)],
-        [((2 * OWN, 1, STATIONS), F32), pltpu.SemaphoreType.DMA],
+        [((4, 8, 8, LANES), F32)],
+        [((2 * OWN, 1, STATIONS), F32), ((4, 8, 8, LANES), F32), pltpu.SemaphoreType.DMA((5,))],
         "turn",
+        [hbm],
         [hbm],
     )(held(visibilities.reshape(2 * OWN, 1, STATIONS)))
     slots = [s ^ LEAD for s in range(STATIONS // OWN)]
-    tiles = lax.all_to_all(tiles, "stcol", 0, 0, tiled=True, axis_index_groups=[slots]).reshape(STATIONS // 2, LANES)
+    tiles = lax.all_to_all(tiles.reshape(STATIONS // OWN, 8, LANES), "stcol", 0, 0, tiled=True, axis_index_groups=[slots]).reshape(STATIONS // 2, LANES)
     count = DIRS * SRC
     model, own, table, gains, pred, den, pen = called(
         model_kernel,

time: 72.5 us -> 72.5 us (level)
  no operation moved by 1% of the time
where the time goes in v7:
time: 72.5 us; the launch traced here: 72 us
  starting transfers between devices  27.6 us (38%)
  blocking collectives  25.7 us (35%)
  Pallas kernels  14.1 us (19%)
  waiting for transfers between devices  3.3 us (5%)
    all_to_all x3, blocking collectives, to_all(): lax.all_to_all(tiles, axis, 0, 0, tiled=True, axis_index_groups=groups)  25.7 us
    all_to_all x1, starting transfers between devices, on_device(): lax.all_to_all(tiles.reshape(STATIONS // OWN, 8, LANES), 'stcol', 0, 0, t...  12.6 us
    pallas_call x1, Pallas kernels, on_device(): called(model_kernel, [model_out, state_out, ((STATIONS, STATIONS), BF16),...  6.93 us
    all_to_all x1, starting transfers between devices, to_all(): lax.all_to_all(tiles, axis, 0, 0, tiled=True, axis_index_groups=groups)  6.63 us
    ppermute x1, starting transfers between devices, both_cores(): lax.ppermute(near, 'freq', [(i, i ^ 1) for i in range(CHANNELS)])  4.92 us
    ppermute x3, starting transfers between devices, around(): lax.ppermute(tile, 'freq', [(i, i ^ 2 * d) for i in range(CHANNELS)])  3.41 us
    ppermute x3, waiting for transfers between devices, around(): lax.ppermute(tile, 'freq', [(i, i ^ 2 * d) for i in range(CHANNELS)])  3.29 us
    pallas_call x1, Pallas kernels, on_device(): called(turn_kernel, [((4, 8, 8, LANES), F32)], [((2 * OWN, 1, STATIONS),...  1.68 us
  transfers between devices with their start and end apart: 6, of which 2 were waited for; matrix products, arithmetic and copies ran while one was open for 0% of the time, Pallas kernels for 11%

profile of v7, /device:TPU:1, one launch (start us, length us, event | category | flops | bytes accessed | tf_op | source)
XLA Modules:
  0.0 72.0 jit_solution(10179986153654839404)
XLA Ops:
  0.6 1.7 %turn.1 = f32[4,8,8,128]{3,2,1,0:T(8,128)} custom-call(f32[32,1,512]{2,1,0:T(1,128)} %bitcast.26), custom_call_target="tpu_custom_call" | custom-call | tf_op jit(solution)/shard_map/turn/pallas_call | solution.py:501
  2.3 12.6 %all-to-all-start = ((f32[32,8,128]{2,1,0:T(8,128)}), f32[32,8,128]{2,1,0:T(8,128)S(1)}, u32[]{:S(2)}, u32[]{:S(2)}) async-start(f32[32,8,128]{2,1,0:T(8,128)} %bitcast.6), calls=%async_computation | async-start | bytes 262144 | tf_op jit(solution)/shard_map/all_to_all | solution.py:510
  14.9 6.9 %models.1 = (f32[16,64,512]{2,1,0:T(8,128)S(1)}, f32[32,128]{1,0:T(8,128)S(1)}, bf16[512,512]{1,0:T(8,128)(2,1)S(1)}, f32[32,512]{1,0:T(8,128)S(1)}, f32[64,512]...) custom-call(f32[32,512]{1,0:T(8,128)} %bitcast.27, f32[3,1,512]{2,1,0:T(1,128)} %place_hbm.1, ...), custom_call_target="tpu_custom_call" | custom-call | tf_op jit(solution)/shard_map/models/pallas_call | solution.py:512
  21.8 0.0 all-to-all-done
  21.9 1.1 %pass_one.1 = (f32[64,512]{1,0:T(8,128)S(1)}, f32[32,128]{1,0:T(8,128)S(1)}, f32[8,128]{1,0:T(8,128)S(1)}) custom-call(f32[256,128]{1,0:T(8,128)S(1)} %bitcast.21, bf16[512,512]{1,0:T(8,128)(2,1)S(1)} %get-tuple-element.29.table_ref, f32[16,64,512]{2,1,0:T(8,128)S(1)} %get-tuple-element.28.model_ref, f32[32,512]{1,0:T(8,128)S(1)} %get-tuple-element.30.gains_ref, ...), custom_call_target="tpu_custom_call" | custom-call | tf_op jit(solution)/shard_map/pass_one/pallas_call | solution.py:526
  23.0 9.5 %all_to_all.25 = f32[16,8,128]{2,1,0:T(8,128)S(1)} all-to-all(f32[16,8,128]{2,1,0:T(8,128)S(1)} %broadcast_in_dim.12), channel_id=1, replica_groups={{18,19,16,17,26,27,24,25,2,3,0,1,10,11,8,9},{22,23,20,21,30,31,28,29,6,..., dimensions={0} | all-to-all | bytes 131072 | tf_op jit(solution)/shard_map/all_to_all | solution.py:471
  32.5 1.3 %pass_two.1 = (f32[32,128]{1,0:T(8,128)S(1)}, f32[8,128]{1,0:T(8,128)S(1)}) custom-call(f32[16,64,512]{2,1,0:T(8,128)S(1)} %get-tuple-element.28.model_ref, f32[64,512]{1,0:T(8,128)S(1)} %get-tuple-element.35.vis_ref, f32[128,128]{1,0:T(8,128)S(1)} %bitcast.24, f32[32,128]{1,0:T(8,128)S(1)} %get-tuple-element.37.own_ref, ...), custom_call_target="tpu_custom_call" | custom-call | tf_op jit(solution)/shard_map/pass_two/pallas_call | solution.py:530
  33.8 0.6 broadcast_in_dim.13
  34.5 6.6 %all-to-all-start.2 = ((f32[16,8,128]{2,1,0:T(8,128)}), f32[16,8,128]{2,1,0:T(8,128)S(1)}, u32[]{:S(2)}, u32[]{:S(2)}) async-start(f32[16,8,128]{2,1,0:T(8,128)} %broadcast_in_dim.13), calls=%async_computation.2 | async-start | bytes 131072 | tf_op jit(solution)/shard_map/all_to_all | solution.py:471
  41.1 2.7 %collective-permute-start.2 = (f32[8,128]{1,0:T(8,128)S(1)}, f32[8,128]{1,0:T(8,128)S(1)}, u32[]{:S(2)}, u32[]{:S(2)}) collective-permute-start(f32[8,128]{1,0:T(8,128)S(1)} %get-tuple-element.42), channel_id=1, source_target_pairs={{0,192},{32,224},{64,128},{96,160},{128,64},{160,96},{192,0},{224,... | collective-permute-start | bytes 12296 | tf_op jit(solution)/shard_map/ppermute | solution.py:475
  43.9 0.3 collective-permute-start.1
  44.2 0.3 collective-permute-start
  44.5 0.6 collective-permute-done.2
  45.1 2.7 %collective-permute-done.1 = f32[8,128]{1,0:T(8,128)S(1)} collective-permute-done((f32[8,128]{1,0:T(8,128)S(1)}, f32[8,128]{1,0:T(8,128)S(1)}, u32[]{:S(2)}, u32[]{:S(2)}) %collective-permute-start.1) | collective-permute-done | bytes 4128 | tf_op jit(solution)/shard_map/ppermute | solution.py:475
  47.8 0.0 collective-permute-done
  47.8 0.0 all-to-all-done.2
  47.8 4.9 %collective-permute-start.3 = (f32[4,8,128]{2,1,0:T(8,128)S(1)}, f32[4,8,128]{2,1,0:T(8,128)S(1)}, u32[]{:S(2)}, u32[]{:S(2)}) collective-permute-start(f32[4,8,128]{2,1,0:T(8,128)S(1)} %pad_maximum_fusion.near_ref), channel_id=1, source_target_pairs={{0,32},{32,0},{64,96},{96,64},{128,160},{160,128},{192,224},{224,1... | collective-permute-start | bytes 49160 | tf_op jit(solution)/shard_map/ppermute | solution.py:481
  52.8 1.2 %pass_three.1 = (f32[32,128]{1,0:T(8,128)S(1)}, f32[32,128]{1,0:T(8,128)S(1)}) custom-call(f32[16,64,512]{2,1,0:T(8,128)S(1)} %get-tuple-element.28.model_ref, f32[64,512]{1,0:T(8,128)S(1)} %get-tuple-element.35.vis_ref, f32[128,128]{1,0:T(8,128)S(1)} %bitcast.22, f32[32,128]{1,0:T(8,128)S(1)} %get-tuple-element.39.own_ref), custom_call_target="tpu_custom_call" | custom-call | tf_op jit(solution)/shard_map/pass_three/pallas_call | solution.py:535
  54.0 0.0 collective-permute-done.3.far_ref
  54.0 0.2 update_three.1
  54.2 8.6 %all_to_all.26 = f32[16,8,128]{2,1,0:T(8,128)S(1)} all-to-all(f32[16,8,128]{2,1,0:T(8,128)S(1)} %broadcast_in_dim.14), channel_id=1, replica_groups={{18,19,16,17,26,27,24,25,2,3,0,1,10,11,8,9},{22,23,20,21,30,31,28,29,6,..., dimensions={0} | all-to-all | bytes 131072 | tf_op jit(solution)/shard_map/all_to_all | solution.py:471
  62.9 0.9 %pass_four.1 = (f32[16,128]{1,0:T(8,128)S(1)}, f32[4,128]{1,0:T(4,128)S(1)}) custom-call(f32[16,64,512]{2,1,0:T(8,128)S(1)} %get-tuple-element.28.model_ref, f32[64,512]{1,0:T(8,128)S(1)} %get-tuple-element.35.vis_ref, f32[128,128]{1,0:T(8,128)S(1)} %bitcast.23, f32[32,128]{1,0:T(8,128)S(1)} %get-tuple-element.47.own_ref, ...), custom_call_target="tpu_custom_call" | custom-call | tf_op jit(solution)/shard_map/pass_four/pallas_call | solution.py:541
  63.7 7.6 %all_to_all.27.tiles_ref = f32[8,4,128]{2,1,0:T(4,128)S(1)} all-to-all(f32[8,4,128]{2,1,0:T(4,128)S(1)} %broadcast_in_dim.15), channel_id=1, replica_groups={{128,160,192,224,0,32,64,96},{129,161,193,225,1,33,65,97},{130,162,194,..., dimensions={0} | all-to-all | bytes 32768 | tf_op jit(solution)/shard_map/all_to_all | solution.py:471
  71.3 0.8 %consensus.1 = (f32[32,16]{1,0:T(8,128)}, f32[32,16]{1,0:T(8,128)}) custom-call(f32[8,4,128]{2,1,0:T(4,128)S(1)} %all_to_all.27.tiles_ref, f32[16,128]{1,0:T(8,128)S(1)} %get-tuple-element.51.state_ref), custom_call_target="tpu_custom_call" | custom-call | tf_op jit(solution)/shard_map/consensus/pallas_call | solution.py:544
  (4 shorter events, 0.0 us)
Async XLA Ops:
  2.3 19.5 %all-to-all-start = ((f32[32,8,128]{2,1,0:T(8,128)}), f32[32,8,128]{2,1,0:T(8,128)S(1)}, u32[]{:S(2)}, u32[]{:S(2)}) async-start(f32[32,8,128]{2,1,0:T(8,128)} %bitcast.6), calls=%async_computation | async-start | bytes 262144 | tf_op jit(solution)/shard_map/all_to_all | solution.py:510
  34.5 13.3 %all-to-all-start.2 = ((f32[16,8,128]{2,1,0:T(8,128)}), f32[16,8,128]{2,1,0:T(8,128)S(1)}, u32[]{:S(2)}, u32[]{:S(2)}) async-start(f32[16,8,128]{2,1,0:T(8,128)} %broadcast_in_dim.13), calls=%async_computation.2 | async-start | bytes 131072 | tf_op jit(solution)/shard_map/all_to_all | solution.py:471
  41.1 4.0 %collective-permute-start.2 = (f32[8,128]{1,0:T(8,128)S(1)}, f32[8,128]{1,0:T(8,128)S(1)}, u32[]{:S(2)}, u32[]{:S(2)}) collective-permute-start(f32[8,128]{1,0:T(8,128)S(1)} %get-tuple-element.42), channel_id=1, source_target_pairs={{0,192},{32,224},{64,128},{96,160},{128,64},{160,96},{192,0},{224,... | collective-permute-start | bytes 12296 | tf_op jit(solution)/shard_map/ppermute | solution.py:475
  43.9 4.0 %collective-permute-start.1 = (f32[8,128]{1,0:T(8,128)S(1)}, f32[8,128]{1,0:T(8,128)S(1)}, u32[]{:S(2)}, u32[]{:S(2)}) collective-permute-start(f32[8,128]{1,0:T(8,128)S(1)} %get-tuple-element.42), channel_id=1, source_target_pairs={{0,128},{32,160},{64,192},{96,224},{128,0},{160,32},{192,64},{224,... | collective-permute-start | bytes 12296 | tf_op jit(solution)/shard_map/ppermute | solution.py:475
  44.2 3.6 %collective-permute-start = (f32[8,128]{1,0:T(8,128)S(1)}, f32[8,128]{1,0:T(8,128)S(1)}, u32[]{:S(2)}, u32[]{:S(2)}) collective-permute-start(f32[8,128]{1,0:T(8,128)S(1)} %get-tuple-element.42), channel_id=1, source_target_pairs={{0,64},{32,96},{64,0},{96,32},{128,192},{160,224},{192,128},{224,1... | collective-permute-start | bytes 12296 | tf_op jit(solution)/shard_map/ppermute | solution.py:475
  47.8 6.2 %collective-permute-start.3 = (f32[4,8,128]{2,1,0:T(8,128)S(1)}, f32[4,8,128]{2,1,0:T(8,128)S(1)}, u32[]{:S(2)}, u32[]{:S(2)}) collective-permute-start(f32[4,8,128]{2,1,0:T(8,128)S(1)} %pad_maximum_fusion.near_ref), channel_id=1, source_target_pairs={{0,32},{32,0},{64,96},{96,64},{128,160},{160,128},{192,224},{224,1... | collective-permute-start | bytes 49160 | tf_op jit(solution)/shard_map/ppermute | solution.py:481
